TPU v7x, 256 devices: a whole 4x4x8 slice. The times are simulated.
256 devices in a mesh: leaf: 256 (over x, z, y, core).
Axes of the slice: x: 4, y: 4, z: 8, core: 2. Of those that a mesh axis runs over, the one named last changes fastest.
Arguments:
- near_blocks: bfloat16 [512, 26, 256, 256], P('leaf'), may hold values from -0.0582 to 0.0582
- diag_blocks: bfloat16 [512, 256, 256], P('leaf'), as said below
- bases: bfloat16 [512, 256, 256], P('leaf'), as said below
- leaf_nbrs: int32 [512, 26], P('leaf'), may hold values from -1 to 511, as said below
- parent_nbrs: int32 [64, 5], replicated, may hold values from 0 to 63, as said below
Outputs:
- leaf_factor: float32 [512, 128, 128], P('leaf')
- leaf_panel: float32 [512, 128, 128], P('leaf')
- merged: float32 [512, 5, 128, 1024], P('leaf')
- parent_block: float32 [65536, 1024], P('leaf')
Inputs may be any that keep to these rules, and one draw needn't show every extreme that they name: `leaf_nbrs`: row i lists distinct leaves j with j != i and |j - i| <= 16; live entries come first and -1 fills the rest; every row has at least 13 live entries and some row has all 26. `parent_nbrs`: row P begins with P itself, followed by the other 4 parents nearest to P in numbering, distinct, equally near ones in any order. `diag_blocks`: each block is symmetric positive definite. `bases`: each basis is an orthogonal matrix rounded to bfloat16.
All inputs are finite; a program needn't handle non-finite values.
Results may differ from a plain program's by a relative error of at most 0.001.
The roundings to bfloat16 on the way count: a program that leaves them out, or rounds other values in their place, can miss the bound.
Values may be sent and summed in bfloat16 or wider, within the bound.
No kernel may reach another device: no remote copies, remote signals or barrier semaphores. Data moves between devices by JAX's collectives and lax.ppermute only.
A program may use at most 128 MiB of HBM per device.

v0:
```python
import jax
import jax.numpy as jnp
from jax import lax
from jax.sharding import PartitionSpec as P

RANK = 128
REACH = 16
CHILDREN = 8


highest = lax.Precision.HIGHEST


def shortened(value):

    def short(part):
        return part.astype(jnp.bfloat16) if part.dtype == jnp.float32 else part

    return jax.tree.map(short, value)


def passed_along(value, axis, steps):
    count = lax.axis_size(axis)
    leading, last = (max(0, -steps), min(count, count - steps))
    return lax.ppermute(value, axis, [(source, source + steps) for source in range(leading, last)])


def partner_2(value, axis, apart):
    mask = 2**apart
    pairs = [(source, source ^ mask) for source in range(lax.axis_size(axis))]
    return lax.ppermute(value, axis, pairs)


def lower_solve(lower_factor, right_side):
    return lax.linalg.triangular_solve(lower_factor, right_side, left_side=True, lower=True)


def back_solve(lower_factor, right_side):
    return lax.linalg.triangular_solve(
        lower_factor, right_side, left_side=True, lower=True, transpose_a=True
    )


def flatten_front(tensor):
    return tensor.reshape((tensor.shape[0] * tensor.shape[1],) + tensor.shape[2:])


def join_front(head_part, tail_part):
    return jnp.concatenate([head_part, tail_part])


def local(near_blocks, diag_blocks, bases, leaf_nbrs, parent_nbrs):
    per_device = bases.shape[0]
    leaf_rows = bases.shape[1]
    redundant = leaf_rows - RANK
    device = lax.axis_index("leaf")
    span_dev = REACH // per_device
    half_diag = jnp.einsum(
        "lba,lbc->lac", bases, diag_blocks, preferred_element_type=jnp.float32
    ).astype(jnp.bfloat16)
    dense_diag = jnp.einsum("lac,lcb->lab", half_diag, bases, preferred_element_type=jnp.float32)
    leaf_factor = jnp.linalg.cholesky(dense_diag[:, :redundant, :redundant])
    leaf_panel = lower_solve(leaf_factor, dense_diag[:, :redundant, redundant:])
    skeleton = dense_diag[:, redundant:, redundant:] - jnp.einsum(
        "lka,lkb->lab", leaf_panel, leaf_panel, precision=highest
    )
    leaf_shift = lax.optimization_barrier(back_solve(leaf_factor, leaf_panel).astype(jnp.bfloat16))
    package = (bases, leaf_shift)
    half_proj = jnp.einsum(
        "lba,lnbc->lnac", bases, near_blocks, preferred_element_type=jnp.float32
    ).astype(jnp.bfloat16)
    lower_side = jax.tree.map(lambda tensor: tensor[None], package)
    upper_side = lower_side
    covered = 0
    while covered < span_dev:
        stride = covered + 1
        amount = min(stride, span_dev - covered)
        outgoing_low = jax.tree.map(lambda tensor: tensor[:amount], lower_side)
        outgoing_high = jax.tree.map(lambda tensor: tensor[:amount], upper_side)
        incoming_low = jax.tree.map(
            lambda part, own: part.astype(own.dtype),
            passed_along(shortened(outgoing_low), "leaf", stride),
            outgoing_low,
        )
        incoming_high = jax.tree.map(
            lambda part, own: part.astype(own.dtype),
            passed_along(shortened(outgoing_high), "leaf", -stride),
            outgoing_high,
        )
        lower_side = jax.tree.map(join_front, lower_side, incoming_low)
        upper_side = jax.tree.map(join_front, upper_side, incoming_high)
        covered = covered + amount
    window = jax.tree.map(
        lambda head_part, tail_part: jnp.concatenate([head_part[::-1], tail_part[1:]]),
        lower_side,
        upper_side,
    )
    win_bases, win_shift = jax.tree.map(flatten_front, window)
    leaf_ids = device * per_device + jnp.arange(per_device, dtype=jnp.int32)
    is_live = leaf_nbrs >= 0
    clipped = jnp.maximum(leaf_nbrs, 0)
    window_slot = (clipped // per_device - device + span_dev) * per_device + clipped % per_device
    window_slot = jnp.clip(window_slot, 0, (2 * span_dev + 1) * per_device - 1)
    near_bases = win_bases[window_slot]
    near_shift = win_shift[window_slot].astype(jnp.float32)
    own_shift = leaf_shift.astype(jnp.float32)
    coupled = jnp.einsum(
        "lnac,lncb->lnab", half_proj, near_bases, preferred_element_type=jnp.float32
    )
    first_term = jnp.einsum(
        "lka,lnkb->lnab", own_shift, coupled[:, :, :redundant, redundant:], precision=highest
    )
    second_term = jnp.einsum(
        "lnak,lnkb->lnab", coupled[:, :, redundant:, :redundant], near_shift, precision=highest
    )
    near_schur = jnp.where(
        is_live[:, :, None, None],
        coupled[:, :, redundant:, redundant:] - first_term - second_term,
        jnp.float32(0.0),
    )
    children = jnp.arange(CHILDREN, dtype=jnp.int32)
    parent = leaf_ids // CHILDREN
    position = leaf_ids % CHILDREN
    parent_count = parent_nbrs.shape[0]
    selector = (jnp.arange(parent_count, dtype=jnp.int32)[None, :] == parent[:, None]).astype(
        jnp.int32
    )
    targets = jnp.sum(selector[:, :, None] * parent_nbrs[None, :, :], axis=1)
    slot_hits = (
        is_live[:, None, None, :]
        & (clipped[:, None, None, :] // CHILDREN == targets[:, :, None, None])
        & (clipped[:, None, None, :] % CHILDREN == children[None, None, :, None])
    )
    self_hit = (targets[:, :, None] == parent[:, None, None]) & (
        children[None, None, :] == position[:, None, None]
    )
    parent_rows = jnp.einsum(
        "lqbn,lnxy->lqxby", slot_hits.astype(jnp.float32), near_schur, precision=highest
    )
    parent_rows = (
        parent_rows
        + self_hit.astype(jnp.float32)[:, :, None, :, None] * skeleton[:, None, :, None, :]
    )
    merged = parent_rows.reshape(parent_rows.shape[0], parent_rows.shape[1], RANK, CHILDREN * RANK)
    own_rows = merged[:, 0].reshape(per_device * RANK, CHILDREN * RANK)
    group_size = CHILDREN // per_device
    group_place = device % group_size
    gathered = own_rows
    for bit_number in range(group_size.bit_length() - 1):
        partner = partner_2(gathered.astype(jnp.bfloat16), "leaf", bit_number).astype(
            gathered.dtype
        )
        is_upper = device // (1 << bit_number) % 2 == 1
        gathered = jnp.where(
            is_upper, jnp.concatenate([partner, gathered]), jnp.concatenate([gathered, partner])
        )
    own_columns = lax.dynamic_slice_in_dim(
        gathered, group_place * per_device * RANK, per_device * RANK, 1
    )
    parent_block = 0.5 * (own_rows + own_columns.T)
    return (leaf_factor, leaf_panel, merged, parent_block)


def solution(mesh):
    in_specs = (
        P("leaf", None, None, None),
        P("leaf", None, None),
        P("leaf", None, None),
        P("leaf", None),
        P(),
    )
    out_specs = (
        P("leaf", None, None),
        P("leaf", None, None),
        P("leaf", None, None, None),
        P("leaf", None),
    )
    return jax.shard_map(local, mesh=mesh, in_specs=in_specs, out_specs=out_specs, check_vma=False)
```

profile of v0, /device:TPU:7, one launch (start us, length us, event | category | flops | bytes accessed | tf_op | source)
XLA Modules:
  0.0 245.7 jit_solution(2680016365966828315)
XLA Ops:
  0.7 3.9 %collective-permute-start = (bf16[1,2,256,256]{3,2,1,0:T(8,128)(2,1)}, bf16[1,2,256,256]{3,2,1,0:T(8,128)(2,1)S(1)}, u32[]{:S(2)}, u32[]{:S(2)}) collective-permute-start(bf16[1,2,256,256]{3,2,1,0:T(8,128)(2,1)} %bitcast.62), channel_id=1, source_target_pairs={{0,1},{1,2},{2,3},{3,4},{4,5},{5,6},{6,7},{7,8},{8,9},{9,10},{10,1... | collective-permute-start | bytes 786440 | tf_op jit(solution)/shard_map/ppermute | solution.py:25
  4.6 1.9 collective-permute-start.4
  6.5 3.5 %collective-permute-start.3 = (bf16[1,2,256,256]{3,2,1,0:T(8,128)(2,1)}, bf16[1,2,256,256]{3,2,1,0:T(8,128)(2,1)}, u32[]{:S(2)}, u32[]{:S(2)}) collective-permute-start(bf16[1,2,256,256]{3,2,1,0:T(8,128)(2,1)} %bitcast.64), channel_id=1, source_target_pairs={{0,8},{1,9},{2,10},{3,11},{4,12},{5,13},{6,14},{7,15},{8,16},{9,17... | collective-permute-start | bytes 786440 | tf_op jit(solution)/shard_map/ppermute | solution.py:25
  11.7 23.5 %custom-call.9 = f32[2,128,128]{2,1,0:T(8,128)S(1)} custom-call(f32[2,128,128]{2,1,0:T(8,128)S(1)} %fusion.34), custom_call_target="Cholesky" | custom-call | tf_op jit(solution)/shard_map/jit(cholesky)/cholesky | solution.py:62
  36.1 19.7 %custom-call.10 = f32[2,1,128,128]{2,3,1,0:T(8,128)S(1)} custom-call(f32[2,1,128,128]{3,2,1,0:T(8,128)S(1)} %get-tuple-element.22), custom_call_target="InvertDiagBlocksLowerTriangular" | custom-call | tf_op jit(solution)/shard_map/triangular_solve | solution.py:35
  56.4 3.9 %collective-permute-start.8 = (bf16[1,2,128,128]{3,2,1,0:T(8,128)(2,1)S(1)}, bf16[1,2,128,128]{3,2,1,0:T(8,128)(2,1)S(1)}, u32[]{:S(2)}, u32[]{:S(2)}) collective-permute-start(bf16[1,2,128,128]{3,2,1,0:T(8,128)(2,1)S(1)} %bitcast.71), channel_id=1, source_target_pairs={{0,1},{1,2},{2,3},{3,4},{4,5},{5,6},{6,7},{7,8},{8,9},{9,10},{10,1... | collective-permute-start | bytes 196616 | tf_op jit(solution)/shard_map/ppermute | solution.py:25
  60.3 5.1 %collective-permute-start.12 = (bf16[1,2,128,128]{3,2,1,0:T(8,128)(2,1)S(1)}, bf16[1,2,128,128]{3,2,1,0:T(8,128)(2,1)S(1)}, u32[]{:S(2)}, u32[]{:S(2)}) collective-permute-start(bf16[1,2,128,128]{3,2,1,0:T(8,128)(2,1)S(1)} %bitcast.72), channel_id=1, source_target_pairs={{1,0},{2,1},{3,2},{4,3},{5,4},{6,5},{7,6},{8,7},{9,8},{10,9},{11,1... | collective-permute-start | bytes 196616 | tf_op jit(solution)/shard_map/ppermute | solution.py:25
  70.7 7.6 %collective-permute-start.5 = (bf16[2,2,256,256]{3,2,1,0:T(8,128)(2,1)S(1)}, bf16[2,2,256,256]{3,2,1,0:T(8,128)(2,1)S(1)}, u32[]{:S(2)}, u32[]{:S(2)}) collective-permute-start(bf16[2,2,256,256]{3,2,1,0:T(8,128)(2,1)S(1)} %get-tuple-element.26), channel_id=1, source_target_pairs={{2,0},{3,1},{4,2},{5,3},{6,4},{7,5},{8,6},{9,7},{10,8},{11,9},{12,... | collective-permute-start | bytes 1572872 | tf_op jit(solution)/shard_map/ppermute | solution.py:25
  78.3 1.9 collective-permute-start.9
  80.3 7.6 %collective-permute-start.13 = (bf16[2,2,128,128]{3,2,1,0:T(8,128)(2,1)S(1)}, bf16[2,2,128,128]{3,2,1,0:T(8,128)(2,1)S(1)}, u32[]{:S(2)}, u32[]{:S(2)}) collective-permute-start(bf16[2,2,128,128]{3,2,1,0:T(8,128)(2,1)S(1)} %get-tuple-element.30), channel_id=1, source_target_pairs={{2,0},{3,1},{4,2},{5,3},{6,4},{7,5},{8,6},{9,7},{10,8},{11,9},{12,... | collective-permute-start | bytes 393224 | tf_op jit(solution)/shard_map/ppermute | solution.py:25
  87.9 2.1 collective-permute-done.9
  92.0 3.4 %collective-permute-start.11 = (bf16[1,2,128,128]{3,2,1,0:T(8,128)(2,1)S(1)}, bf16[1,2,128,128]{3,2,1,0:T(8,128)(2,1)S(1)}, u32[]{:S(2)}, u32[]{:S(2)}) collective-permute-start(bf16[1,2,128,128]{3,2,1,0:T(8,128)(2,1)S(1)} %bitcast.74), channel_id=1, source_target_pairs={{0,8},{1,9},{2,10},{3,11},{4,12},{5,13},{6,14},{7,15},{8,16},{9,17... | collective-permute-start | bytes 196616 | tf_op jit(solution)/shard_map/ppermute | solution.py:25
  98.9 4.6 %collective-permute-start.2 = (bf16[4,2,256,256]{3,2,1,0:T(8,128)(2,1)}, bf16[4,2,256,256]{3,2,1,0:T(8,128)(2,1)}, u32[]{:S(2)}, u32[]{:S(2)}) collective-permute-start(bf16[4,2,256,256]{3,2,1,0:T(8,128)(2,1)} %get-tuple-element.25), channel_id=1, source_target_pairs={{0,4},{1,5},{2,6},{3,7},{4,8},{5,9},{6,10},{7,11},{8,12},{9,13},{1... | collective-permute-start | bytes 3145736 | tf_op jit(solution)/shard_map/ppermute | solution.py:25
  104.2 2.9 %collective-permute-done.10 = bf16[4,2,128,128]{3,2,1,0:T(8,128)(2,1)S(1)} collective-permute-done((bf16[4,2,128,128]{3,2,1,0:T(8,128)(2,1)S(1)}, bf16[4,2,128,128]{3,2,1,0:T(8,128)(2,1)S(1)}, u32[]{:S(2)}, u32[]{:S(2)}) %collective-permute-start.10) | collective-permute-done | bytes 262176 | tf_op jit(solution)/shard_map/ppermute | solution.py:25
  107.1 2.3 collective-permute-start.14
  109.5 4.9 %collective-permute-start.6 = (bf16[4,2,256,256]{3,2,1,0:T(8,128)(2,1)}, bf16[4,2,256,256]{3,2,1,0:T(8,128)(2,1)}, u32[]{:S(2)}, u32[]{:S(2)}) collective-permute-start(bf16[4,2,256,256]{3,2,1,0:T(8,128)(2,1)} %get-tuple-element.24), channel_id=1, source_target_pairs={{4,0},{5,1},{6,2},{7,3},{8,4},{9,5},{10,6},{11,7},{12,8},{13,9},{1... | collective-permute-start | bytes 3145736 | tf_op jit(solution)/shard_map/ppermute | solution.py:25
  114.4 24.5 %collective-permute-done.14 = bf16[4,2,128,128]{3,2,1,0:T(8,128)(2,1)S(1)} collective-permute-done((bf16[4,2,128,128]{3,2,1,0:T(8,128)(2,1)S(1)}, bf16[4,2,128,128]{3,2,1,0:T(8,128)(2,1)S(1)}, u32[]{:S(2)}, u32[]{:S(2)}) %collective-permute-start.14) | collective-permute-done | bytes 262176 | tf_op jit(solution)/shard_map/ppermute | solution.py:25
  139.0 2.1 collective-permute-start.15
  141.2 3.2 %collective-permute-done.15 = bf16[1,2,128,128]{3,2,1,0:T(8,128)(2,1)S(1)} collective-permute-done((bf16[1,2,128,128]{3,2,1,0:T(8,128)(2,1)S(1)}, bf16[1,2,128,128]{3,2,1,0:T(8,128)(2,1)S(1)}, u32[]{:S(2)}, u32[]{:S(2)}) %collective-permute-start.15) | collective-permute-done | bytes 65568 | tf_op jit(solution)/shard_map/ppermute | solution.py:25
  147.2 7.3 %collective-permute-done.2 = bf16[4,2,256,256]{3,2,1,0:T(8,128)(2,1)} collective-permute-done((bf16[4,2,256,256]{3,2,1,0:T(8,128)(2,1)}, bf16[4,2,256,256]{3,2,1,0:T(8,128)(2,1)}, u32[]{:S(2)}, u32[]{:S(2)}) %collective-permute-start.2) | collective-permute-done | bytes 1048608 | tf_op jit(solution)/shard_map/ppermute | solution.py:25
  154.5 2.3 constant_dynamic-update-slice_fusion.1
  158.5 3.3 %reverse_dynamic-update-slice_fusion = bf16[17,2,256,256]{3,2,1,0:T(8,128)(2,1)} fusion(bf16[9,2,256,256]{3,2,1,0:T(8,128)(2,1)} %constant_dynamic-update-slice_fusion), kind=kLoop, calls=%fused_computation.20 | loop fusion | bytes 4718592
  163.4 2.3 constant_dynamic-update-slice_fusion.6
  167.3 7.3 %gather_fusion = bf16[52,256,256]{2,1,0:T(8,128)(2,1)} fusion(bf16[34,256,256]{2,1,0:T(8,128)(2,1)} %bitcast.6, s32[1024]{0:T(1024)S(1)} %pad_clamp_fusion), kind=kCustom, calls=%fused_computation | custom fusion | bytes 13631696 | tf_op jit(solution)/shard_map/gather | solution.py:104
  174.6 12.5 %fusion = f32[2,26,256,256]{3,2,1,0:T(8,128)} fusion(bf16[2,26,256,256]{3,2,1,0:T(8,128)(2,1)} %bitcast.59, bf16[2,26,256,256]{3,2,1,0:T(8,128)(2,1)} %param.5, bf16[2,256,256]{2,1,0:T(8,128)(2,1)S(1)} %copy-done.2), kind=kOutput, calls=%fused_computation.2 | convolution fusion | flops 3493068800 | bytes 27525120 | tf_op jit(solution)/shard_map/lnac,lncb->lnab/dot_general | solution.py:107
  187.0 3.9 %fusion.8 = f32[2,26,128,128]{2,3,1,0:T(8,128)S(1)} fusion(f32[2,26,256,256]{3,2,1,0:T(8,128)} %fusion, bf16[2,128,128]{2,1,0:T(8,128)(2,1)S(1)} %convolution_convert_fusion.1), kind=kOutput, calls=%fused_computation.14 | convolution fusion | flops 1308622848 | bytes 6881280 | tf_op jit(solution)/shard_map/lka,lnkb->lnab/dot_general | solution.py:110
  191.0 5.6 %fusion.12 = f32[2,26,128,128,1]{3,2,1,0,4:T(8,128)S(1)} fusion(f32[2,26,256,256]{3,2,1,0:T(8,128)} %fusion, f32[2,26,128,128]{2,3,1,0:T(8,128)S(1)} %fusion.8, bf16[2,26,128,128]{3,2,1,0:T(8,128)(2,1)S(1)} %bitcast.69, pred[2,26]{1,0:T(4,128)(4,1)S(1)} %copy-done.13), kind=kOutput, calls=%fused_computation.19 | convolution fusion | flops 1311178752 | bytes 15335476 | tf_op jit(solution)/shard_map/lnak,lnkb->lnab/dot_general | solution.py:113
  196.6 7.8 %bitcast_add_fusion = f32[2,5,128,8,128]{4,3,1,2,0:T(8,128)} fusion(f32[2,128,128]{2,1,0:T(8,128)S(1)} %copy-done.10, f32[2,5,8]{2,1,0:T(8,128)S(1)} %and_convert_fusion, f32[2,26,128,128,1]{3,2,1,0,4:T(8,128)S(1)} %fusion.12, pred[2,8,26]{2,1,0:T(8,128)(4,1)S(1)} %copy-done.11, pred[2,5,26]{2,1,0:T(8,128)(4,1)S(1)} %compare_and_fusion), kind=kOutput, calls=%fused_computation.5 | convolution fusion | flops 411568160 | bytes 8782820 | tf_op jit(solution)/shard_map/lqbn,lnxy->lqxby/dot_general | solution.py:137
  204.5 6.3 %copy.56 = f32[2,5,128,8,128]{2,4,3,1,0:T(8,128)} copy(f32[2,5,128,8,128]{4,3,1,2,0:T(8,128)} %bitcast_add_fusion) | data formatting | bytes 10485760 | tf_op jit(solution)/shard_map/add | solution.py:141
  212.8 3.6 %collective-permute-start.16 = (bf16[256,1024]{0,1:T(8,128)(2,1)S(1)}, bf16[256,1024]{0,1:T(8,128)(2,1)S(1)}, u32[]{:S(2)}, u32[]{:S(2)}) collective-permute-start(bf16[256,1024]{0,1:T(8,128)(2,1)S(1)} %convert_element_type.44), channel_id=1, source_target_pairs={{0,1},{1,0},{2,3},{3,2},{4,5},{5,4},{6,7},{7,6},{8,9},{9,8},{10,11... | collective-permute-start | bytes 1572872 | tf_op jit(solution)/shard_map/ppermute | solution.py:31
  219.7 5.9 %copy.61 = f32[2,5,128,1024]{3,2,1,0:T(8,128)} copy(f32[2,5,128,1024]{2,3,1,0:T(8,128)} %bitcast.61) | data formatting | bytes 10485760
  225.6 18.5 %collective-permute-done.17 = bf16[512,1024]{0,1:T(8,128)(2,1)S(1)} collective-permute-done((bf16[512,1024]{0,1:T(8,128)(2,1)S(1)}, bf16[512,1024]{0,1:T(8,128)(2,1)S(1)}, u32[]{:S(2)}, u32[]{:S(2)}) %collective-permute-start.17) | collective-permute-done | bytes 1048608 | tf_op jit(solution)/shard_map/ppermute | solution.py:31
  (104 shorter events, 29.3 us)
Async XLA Ops:
  0.6 9.5 %copy-start = (bf16[2,256,256]{2,1,0:T(8,128)(2,1)S(1)}, bf16[2,256,256]{2,1,0:T(8,128)(2,1)}, u32[]{:S(2)}) copy-start(bf16[2,256,256]{2,1,0:T(8,128)(2,1)} %param.6) | copy-start | bytes 786436
  0.6 64.8 %copy-start.2 = (bf16[2,256,256]{2,1,0:T(8,128)(2,1)S(1)}, bf16[2,256,256]{2,1,0:T(8,128)(2,1)}, u32[]{:S(2)}) copy-start(bf16[2,256,256]{2,1,0:T(8,128)(2,1)} %param.7) | copy-start | bytes 786436
  0.7 65.5 %copy-start.15 = (s32[2,26]{1,0:T(2,128)S(1)}, s32[2,26]{1,0:T(2,128)}, u32[]{:S(2)}) copy-start(s32[2,26]{1,0:T(2,128)} %param.8) | copy-start | bytes 628
  0.7 65.7 %copy-start.14 = (s32[64,5]{0,1:T(8,128)S(1)}, s32[64,5]{0,1:T(8,128)}, u32[]{:S(2)}) copy-start(s32[64,5]{0,1:T(8,128)} %param.9) | copy-start | bytes 3844
  0.7 68.0 %collective-permute-start = (bf16[1,2,256,256]{3,2,1,0:T(8,128)(2,1)}, bf16[1,2,256,256]{3,2,1,0:T(8,128)(2,1)S(1)}, u32[]{:S(2)}, u32[]{:S(2)}) collective-permute-start(bf16[1,2,256,256]{3,2,1,0:T(8,128)(2,1)} %bitcast.62), channel_id=1, source_target_pairs={{0,1},{1,2},{2,3},{3,4},{4,5},{5,6},{6,7},{7,8},{8,9},{9,10},{10,1... | collective-permute-start | bytes 786440 | tf_op jit(solution)/shard_map/ppermute | solution.py:25
  4.6 64.1 %collective-permute-start.4 = (bf16[1,2,256,256]{3,2,1,0:T(8,128)(2,1)}, bf16[1,2,256,256]{3,2,1,0:T(8,128)(2,1)S(1)}, u32[]{:S(2)}, u32[]{:S(2)}) collective-permute-start(bf16[1,2,256,256]{3,2,1,0:T(8,128)(2,1)} %bitcast.63), channel_id=1, source_target_pairs={{1,0},{2,1},{3,2},{4,3},{5,4},{6,5},{7,6},{8,7},{9,8},{10,9},{11,1... | collective-permute-start | bytes 786440 | tf_op jit(solution)/shard_map/ppermute | solution.py:25
  6.5 150.3 %collective-permute-start.3 = (bf16[1,2,256,256]{3,2,1,0:T(8,128)(2,1)}, bf16[1,2,256,256]{3,2,1,0:T(8,128)(2,1)}, u32[]{:S(2)}, u32[]{:S(2)}) collective-permute-start(bf16[1,2,256,256]{3,2,1,0:T(8,128)(2,1)} %bitcast.64), channel_id=1, source_target_pairs={{0,8},{1,9},{2,10},{3,11},{4,12},{5,13},{6,14},{7,15},{8,16},{9,17... | collective-permute-start | bytes 786440 | tf_op jit(solution)/shard_map/ppermute | solution.py:25
  56.1 42.8 %copy-start.9 = (f32[2,128,128]{2,1,0:T(8,128)}, f32[2,128,128]{2,1,0:T(8,128)S(1)}, u32[]{:S(2)}) copy-start(f32[2,128,128]{2,1,0:T(8,128)S(1)} %fusion.30) | copy-start | bytes 393220
  56.4 21.9 %collective-permute-start.8 = (bf16[1,2,128,128]{3,2,1,0:T(8,128)(2,1)S(1)}, bf16[1,2,128,128]{3,2,1,0:T(8,128)(2,1)S(1)}, u32[]{:S(2)}, u32[]{:S(2)}) collective-permute-start(bf16[1,2,128,128]{3,2,1,0:T(8,128)(2,1)S(1)} %bitcast.71), channel_id=1, source_target_pairs={{0,1},{1,2},{2,3},{3,4},{4,5},{5,6},{6,7},{7,8},{8,9},{9,10},{10,1... | collective-permute-start | bytes 196616 | tf_op jit(solution)/shard_map/ppermute | solution.py:25
  60.3 17.9 %collective-permute-start.12 = (bf16[1,2,128,128]{3,2,1,0:T(8,128)(2,1)S(1)}, bf16[1,2,128,128]{3,2,1,0:T(8,128)(2,1)S(1)}, u32[]{:S(2)}, u32[]{:S(2)}) collective-permute-start(bf16[1,2,128,128]{3,2,1,0:T(8,128)(2,1)S(1)} %bitcast.72), channel_id=1, source_target_pairs={{1,0},{2,1},{3,2},{4,3},{5,4},{6,5},{7,6},{8,7},{9,8},{10,9},{11,1... | collective-permute-start | bytes 196616 | tf_op jit(solution)/shard_map/ppermute | solution.py:25
  66.2 12.1 %copy-start.12 = (pred[2,26]{1,0:T(4,128)(4,1)}, pred[2,26]{1,0:T(4,128)(4,1)S(1)}, u32[]{:S(2)}) copy-start(pred[2,26]{1,0:T(4,128)(4,1)S(1)} %broadcast_compare_fusion.1) | copy-start | bytes 160
  68.7 30.2 %copy-start.4 = (bf16[1,2,256,256]{3,2,1,0:T(8,128)(2,1)}, bf16[1,2,256,256]{3,2,1,0:T(8,128)(2,1)S(1)}, u32[]{:S(2)}) copy-start(bf16[1,2,256,256]{3,2,1,0:T(8,128)(2,1)S(1)} %collective-permute-done.4) | copy-start | bytes 786436
  68.7 26.7 %collective-permute-start.1 = (bf16[2,2,256,256]{3,2,1,0:T(8,128)(2,1)S(1)}, bf16[2,2,256,256]{3,2,1,0:T(8,128)(2,1)S(1)}, u32[]{:S(2)}, u32[]{:S(2)}) collective-permute-start(bf16[2,2,256,256]{3,2,1,0:T(8,128)(2,1)S(1)} %get-tuple-element.27), channel_id=1, source_target_pairs={{0,2},{1,3},{2,4},{3,5},{4,6},{5,7},{6,8},{7,9},{8,10},{9,11},{10,... | collective-permute-start | bytes 1572872 | tf_op jit(solution)/shard_map/ppermute | solution.py:25
  70.7 26.7 %collective-permute-start.5 = (bf16[2,2,256,256]{3,2,1,0:T(8,128)(2,1)S(1)}, bf16[2,2,256,256]{3,2,1,0:T(8,128)(2,1)S(1)}, u32[]{:S(2)}, u32[]{:S(2)}) collective-permute-start(bf16[2,2,256,256]{3,2,1,0:T(8,128)(2,1)S(1)} %get-tuple-element.26), channel_id=1, source_target_pairs={{2,0},{3,1},{4,2},{5,3},{6,4},{7,5},{8,6},{9,7},{10,8},{11,9},{12,... | collective-permute-start | bytes 1572872 | tf_op jit(solution)/shard_map/ppermute | solution.py:25
  78.3 11.7 %collective-permute-start.9 = (bf16[2,2,128,128]{3,2,1,0:T(8,128)(2,1)S(1)}, bf16[2,2,128,128]{3,2,1,0:T(8,128)(2,1)S(1)}, u32[]{:S(2)}, u32[]{:S(2)}) collective-permute-start(bf16[2,2,128,128]{3,2,1,0:T(8,128)(2,1)S(1)} %get-tuple-element.31), channel_id=1, source_target_pairs={{0,2},{1,3},{2,4},{3,5},{4,6},{5,7},{6,8},{7,9},{8,10},{9,11},{10,... | collective-permute-start | bytes 393224 | tf_op jit(solution)/shard_map/ppermute | solution.py:25
  80.3 11.7 %collective-permute-start.13 = (bf16[2,2,128,128]{3,2,1,0:T(8,128)(2,1)S(1)}, bf16[2,2,128,128]{3,2,1,0:T(8,128)(2,1)S(1)}, u32[]{:S(2)}, u32[]{:S(2)}) collective-permute-start(bf16[2,2,128,128]{3,2,1,0:T(8,128)(2,1)S(1)} %get-tuple-element.30), channel_id=1, source_target_pairs={{2,0},{3,1},{4,2},{5,3},{6,4},{7,5},{8,6},{9,7},{10,8},{11,9},{12,... | collective-permute-start | bytes 393224 | tf_op jit(solution)/shard_map/ppermute | solution.py:25
  90.0 75.6 %collective-permute-start.7 = (bf16[1,2,256,256]{3,2,1,0:T(8,128)(2,1)S(1)}, bf16[1,2,256,256]{3,2,1,0:T(8,128)(2,1)}, u32[]{:S(2)}, u32[]{:S(2)}) collective-permute-start(bf16[1,2,256,256]{3,2,1,0:T(8,128)(2,1)S(1)} %bitcast.66), channel_id=1, source_target_pairs={{8,0},{9,1},{10,2},{11,3},{12,4},{13,5},{14,6},{15,7},{16,8},{17,9... | collective-permute-start | bytes 786440 | tf_op jit(solution)/shard_map/ppermute | solution.py:25
  92.0 17.5 %collective-permute-start.11 = (bf16[1,2,128,128]{3,2,1,0:T(8,128)(2,1)S(1)}, bf16[1,2,128,128]{3,2,1,0:T(8,128)(2,1)S(1)}, u32[]{:S(2)}, u32[]{:S(2)}) collective-permute-start(bf16[1,2,128,128]{3,2,1,0:T(8,128)(2,1)S(1)} %bitcast.74), channel_id=1, source_target_pairs={{0,8},{1,9},{2,10},{3,11},{4,12},{5,13},{6,14},{7,15},{8,16},{9,17... | collective-permute-start | bytes 196616 | tf_op jit(solution)/shard_map/ppermute | solution.py:25
  95.4 45.7 %copy-start.8 = (bf16[2,2,256,256]{3,2,1,0:T(8,128)(2,1)}, bf16[2,2,256,256]{3,2,1,0:T(8,128)(2,1)S(1)}, u32[]{:S(2)}) copy-start(bf16[2,2,256,256]{3,2,1,0:T(8,128)(2,1)S(1)} %collective-permute-done.1) | copy-start | bytes 1572868
  95.4 11.6 %collective-permute-start.10 = (bf16[4,2,128,128]{3,2,1,0:T(8,128)(2,1)S(1)}, bf16[4,2,128,128]{3,2,1,0:T(8,128)(2,1)S(1)}, u32[]{:S(2)}, u32[]{:S(2)}) collective-permute-start(bf16[4,2,128,128]{3,2,1,0:T(8,128)(2,1)S(1)} %get-tuple-element.29), channel_id=1, source_target_pairs={{0,4},{1,5},{2,6},{3,7},{4,8},{5,9},{6,10},{7,11},{8,12},{9,13},{1... | collective-permute-start | bytes 786440 | tf_op jit(solution)/shard_map/ppermute | solution.py:25
  97.4 43.8 %copy-start.6 = (bf16[2,2,256,256]{3,2,1,0:T(8,128)(2,1)}, bf16[2,2,256,256]{3,2,1,0:T(8,128)(2,1)S(1)}, u32[]{:S(2)}) copy-start(bf16[2,2,256,256]{3,2,1,0:T(8,128)(2,1)S(1)} %collective-permute-done.5) | copy-start | bytes 1572868
  98.9 55.6 %collective-permute-start.2 = (bf16[4,2,256,256]{3,2,1,0:T(8,128)(2,1)}, bf16[4,2,256,256]{3,2,1,0:T(8,128)(2,1)}, u32[]{:S(2)}, u32[]{:S(2)}) collective-permute-start(bf16[4,2,256,256]{3,2,1,0:T(8,128)(2,1)} %get-tuple-element.25), channel_id=1, source_target_pairs={{0,4},{1,5},{2,6},{3,7},{4,8},{5,9},{6,10},{7,11},{8,12},{9,13},{1... | collective-permute-start | bytes 3145736 | tf_op jit(solution)/shard_map/ppermute | solution.py:25
  107.1 31.9 %collective-permute-start.14 = (bf16[4,2,128,128]{3,2,1,0:T(8,128)(2,1)S(1)}, bf16[4,2,128,128]{3,2,1,0:T(8,128)(2,1)S(1)}, u32[]{:S(2)}, u32[]{:S(2)}) collective-permute-start(bf16[4,2,128,128]{3,2,1,0:T(8,128)(2,1)S(1)} %get-tuple-element.28), channel_id=1, source_target_pairs={{4,0},{5,1},{6,2},{7,3},{8,4},{9,5},{10,6},{11,7},{12,8},{13,9},{1... | collective-permute-start | bytes 786440 | tf_op jit(solution)/shard_map/ppermute | solution.py:25
  109.5 53.8 %collective-permute-start.6 = (bf16[4,2,256,256]{3,2,1,0:T(8,128)(2,1)}, bf16[4,2,256,256]{3,2,1,0:T(8,128)(2,1)}, u32[]{:S(2)}, u32[]{:S(2)}) collective-permute-start(bf16[4,2,256,256]{3,2,1,0:T(8,128)(2,1)} %get-tuple-element.24), channel_id=1, source_target_pairs={{4,0},{5,1},{6,2},{7,3},{8,4},{9,5},{10,6},{11,7},{12,8},{13,9},{1... | collective-permute-start | bytes 3145736 | tf_op jit(solution)/shard_map/ppermute | solution.py:25
  139.0 5.4 %collective-permute-start.15 = (bf16[1,2,128,128]{3,2,1,0:T(8,128)(2,1)S(1)}, bf16[1,2,128,128]{3,2,1,0:T(8,128)(2,1)S(1)}, u32[]{:S(2)}, u32[]{:S(2)}) collective-permute-start(bf16[1,2,128,128]{3,2,1,0:T(8,128)(2,1)S(1)} %bitcast.76), channel_id=1, source_target_pairs={{8,0},{9,1},{10,2},{11,3},{12,4},{13,5},{14,6},{15,7},{16,8},{17,9... | collective-permute-start | bytes 196616 | tf_op jit(solution)/shard_map/ppermute | solution.py:25
  147.2 14.6 %copy-start.5 = (bf16[1,2,256,256]{3,2,1,0:T(8,128)(2,1)S(1)}, bf16[1,2,256,256]{3,2,1,0:T(8,128)(2,1)}, u32[]{:S(2)}) copy-start(bf16[1,2,256,256]{3,2,1,0:T(8,128)(2,1)} %copy-done.4) | copy-start | bytes 786436
  156.8 5.7 %copy-start.7 = (bf16[2,2,256,256]{3,2,1,0:T(8,128)(2,1)S(1)}, bf16[2,2,256,256]{3,2,1,0:T(8,128)(2,1)}, u32[]{:S(2)}) copy-start(bf16[2,2,256,256]{3,2,1,0:T(8,128)(2,1)} %copy-done.6) | copy-start | bytes 1572868
  191.0 5.7 %copy-start.10 = (f32[2,128,128]{2,1,0:T(8,128)S(1)}, f32[2,128,128]{2,1,0:T(8,128)}, u32[]{:S(2)}) copy-start(f32[2,128,128]{2,1,0:T(8,128)} %convolution_subtract_fusion) | copy-start | bytes 393220
  191.0 5.7 %copy-start.11 = (pred[2,8,26]{2,1,0:T(8,128)(4,1)S(1)}, pred[2,8,26]{2,1,0:T(8,128)(4,1)}, u32[]{:S(2)}) copy-start(pred[2,8,26]{2,1,0:T(8,128)(4,1)} %iota_compare_fusion.2) | copy-start | bytes 1252
  212.8 5.1 %collective-permute-start.16 = (bf16[256,1024]{0,1:T(8,128)(2,1)S(1)}, bf16[256,1024]{0,1:T(8,128)(2,1)S(1)}, u32[]{:S(2)}, u32[]{:S(2)}) collective-permute-start(bf16[256,1024]{0,1:T(8,128)(2,1)S(1)} %convert_element_type.44), channel_id=1, source_target_pairs={{0,1},{1,0},{2,3},{3,2},{4,5},{5,4},{6,7},{7,6},{8,9},{9,8},{10,11... | collective-permute-start | bytes 1572872 | tf_op jit(solution)/shard_map/ppermute | solution.py:31
  219.7 24.4 %collective-permute-start.17 = (bf16[512,1024]{0,1:T(8,128)(2,1)S(1)}, bf16[512,1024]{0,1:T(8,128)(2,1)S(1)}, u32[]{:S(2)}, u32[]{:S(2)}) collective-permute-start(bf16[512,1024]{0,1:T(8,128)(2,1)S(1)} %get-tuple-element.20), channel_id=1, source_target_pairs={{0,2},{1,3},{2,0},{3,1},{4,6},{5,7},{6,4},{7,5},{8,10},{9,11},{10,... | collective-permute-start | bytes 3145736 | tf_op jit(solution)/shard_map/ppermute | solution.py:31
  225.6 18.8 %copy-start.3 = (f32[512,1024]{0,1:T(8,128)S(1)}, f32[512,1024]{0,1:T(8,128)}, u32[]{:S(2)}) copy-start(f32[512,1024]{0,1:T(8,128)} %get-tuple-element.21) | copy-start | bytes 6291460
  (2 other events, 5.5 us)
where the time goes:
time: 248 us; the launch traced here: 246 us
  starting transfers between devices  62.1 us (25%)
  waiting for transfers between devices  60.2 us (24%)
  other arithmetic  50.2 us (20%)
  local copies, waits for them, and re-layouts  39 us (16%)
  matrix products  32.9 us (13%)
    ppermute x16, starting transfers between devices, passed_along(): lax.ppermute(value, axis, [(source, source + steps) for source in range(l...  58.5 us
    ppermute x16, waiting for transfers between devices, passed_along(): lax.ppermute(value, axis, [(source, source + steps) for source in range(l...  40.2 us
    another operation x4, other arithmetic, local(): leaf_factor = jnp.linalg.cholesky(dense_diag[:, :redundant, :redundant])  23.6 us
    another operation x2, other arithmetic, lower_solve(): lax.linalg.triangular_solve(lower_factor, right_side, left_side=True, low...  20.4 us
    ppermute x2, waiting for transfers between devices, partner_2(): return lax.ppermute(value, axis, pairs)  20 us
    unnamed x50, local copies, waits for them, and re-layouts  18.9 us
    dot_general x1, matrix products, local(): jnp.einsum('lnac,lncb->lnab', half_proj, near_bases, preferred_element_ty...  12.5 us
    dot_general x1, matrix products, local(): jnp.einsum('lqbn,lnxy->lqxby', slot_hits.astype(jnp.float32), near_schur,...  7.8 us
  transfers between devices with their start and end apart: 18, of which 7 were waited for; matrix products, arithmetic and copies ran while one was open for 29% of the time, Pallas kernels for 0%

commit v1 on v0

v1 whole, which is shorter than its diff:
```python
import jax
import jax.numpy as jnp
from jax import lax
from jax.experimental import pallas as pl
from jax.experimental.pallas import tpu as pltpu
from jax.sharding import PartitionSpec as P

RANK = 128
REACH = 16
CHILDREN = 8
SLOTS = 26
PNB = 5
REACH_CHIPS = 4
WINDOW = 36
VMEM = 48 * 1024 * 1024


F32 = jnp.float32
BF = jnp.bfloat16

def split(x):
    hi = x.astype(BF)
    lo = (x - hi.astype(F32)).astype(BF)
    return hi, lo

def dot00(a, b):
    return lax.dot_general(a, b, (((0,), (0,)), ((), ())), preferred_element_type=F32)

def dot00_3(a, b):
    ah, al = split(a); bh, bl = split(b)
    return dot00(jnp.concatenate([ah, ah, al], 0), jnp.concatenate([bh, bl, bh], 0))

def bc(x):
    return jnp.broadcast_to(x, (8, 128))

def eliminate(blocks, out):
    sub = lax.broadcasted_iota(jnp.int32, (8, 128), 0)
    count = len(blocks)
    done = []
    for k in range(count):
        yield
        parts = blocks[k]
        left = parts[0]
        cols = [bc(left[:, 8*k+j:8*k+j+1]) for j in range(8)]
        s = [[bc(cols[j][i:i+1, :]) for j in range(i+1)] for i in range(8)]
        r = [None]*8
        L = [[None]*8 for _ in range(8)]
        for j in range(8):
            r[j] = lax.rsqrt(s[j][j])
            for i in range(j+1, 8):
                L[i][j] = s[i][j]*r[j]
            for i in range(j+1, 8):
                for m in range(j+1, i+1):
                    s[i][m] = s[i][m] - L[i][j]*L[m][j]
        rows = []
        for j in range(8):
            row = []
            for q, part in enumerate(parts):
                x = bc(part[j:j+1, :])
                for m in range(j):
                    x = x - L[j][m]*rows[m][q]
                row.append(x*r[j])
            rows.append(row)
        packed = []
        for q in range(len(parts)):
            x = rows[0][q]
            for j in range(1, 8):
                x = jnp.where(sub == j, rows[j][q], x)
            packed.append(x)
        done.append(packed)
        if k + 1 < count:
            nxt = blocks[k+1]
            cb = [bc(nxt[0][:, 8*k+j:8*k+j+1]) for j in range(8)]
            lc = []
            new = list(nxt)
            for j in range(8):
                x = cb[j]
                for m in range(j):
                    x = x - lc[m]*L[j][m]
                x = x*r[j]
                lc.append(x)
                new = [new[q] - x*rows[j][q] for q in range(len(new))]
            blocks[k+1] = new
        if k + 2 < count:
            wide = jnp.concatenate(packed, 1)
            upd = dot00_3(packed[0], wide)
            for ib in range(k+2, count):
                blocks[ib] = [blocks[ib][q] - upd[8*ib:8*ib+8, 128*q:128*q+128] for q in range(len(packed))]
    out.extend(done)

def k0_body(u_ref, a_ref, f_ref, p_ref, sk_ref, s_ref, d_ref):
    row = lax.broadcasted_iota(jnp.int32, (128, 128), 0)
    col = lax.broadcasted_iota(jnp.int32, (128, 128), 1)
    eye = jnp.where(row == col, 1.0, 0.0).astype(F32)
    outs = []; gens = []
    prep = []
    for l in range(2):
        u = u_ref[l]
        half = dot00(u, a_ref[l]).astype(BF)
        dense = jnp.dot(half, u, preferred_element_type=F32)
        arr = dense[:128, :128]
        arr = 0.5*(arr + arr.T)
        prep.append((u, dense, arr))
    for l in range(2):
        u, dense, arr = prep[l]
        rs = dense[:128, 128:]
        blocks = [[arr[8*i:8*i+8], rs[8*i:8*i+8], eye[8*i:8*i+8]] for i in range(16)]
        outs.append([])
        gens.append(eliminate(blocks, outs[-1]))
    for _ in range(17):
        for g in gens:
            next(g, None)
    for l in range(2):
        u, dense, arr = prep[l]
        done = outs[l]
        upper = jnp.concatenate([d[0] for d in done], 0)
        upper = jnp.where(row <= col, upper, 0.0)
        panel = jnp.concatenate([d[1] for d in done], 0)
        inv = jnp.concatenate([d[2] for d in done], 0)
        f_ref[l] = upper.T
        p_ref[l] = panel
        shift = dot00_3(inv, panel).astype(BF)
        s_ref[l] = shift
        d_ref[l] = jnp.dot(u[:, :128], shift, preferred_element_type=F32).astype(BF)
        sk_ref[l] = dense[128:, 128:] - dot00_3(panel, panel)

def k0(bases, diag):
    sd = jax.ShapeDtypeStruct
    return pl.pallas_call(
        k0_body,
        out_shape=(sd((2,128,128),F32), sd((2,128,128),F32), sd((2,128,128),F32), sd((2,128,128),BF), sd((2,256,128),BF)),
        compiler_params=pltpu.CompilerParams(vmem_limit_bytes=48*1024*1024),
        name="leaf_elimination",
    )(bases, diag)


def window_copies(pieces, win, sems, core):
    own, other = pieces[0], pieces[1]
    copies = []

    def put(src, base, size):
        dst = win.at[pl.ds(base, size)]
        copies.append(pltpu.make_async_copy(src, dst, sems.at[len(copies)]))

    put(own, 16 + 2 * core, 2)
    put(other, 18 - 2 * core, 2)
    for k in range(1, REACH_CHIPS + 1):
        near, far = pieces[2 * k], pieces[2 * k + 1]
        low, high = 4 * (4 - k), 4 * (4 + k)
        put(near, jnp.where(core == 0, low, high), 4)
        put(far, jnp.where(core == 0, high, low), 4)
    return copies


def window_slot(leaf, device):
    pair = device // 2
    below = leaf // 4 < pair
    turned = jnp.where(below, leaf ^ 2, leaf)
    return turned - 4 * pair + REACH


def near_body(nbrs, u_ref, s_ref, a_ref, *refs):
    pieces = refs[:10]
    p1_ref, hs_ref, ut_ref, st_ref, win, sems = refs[10:]
    device = lax.axis_index("leaf")
    leaf, part = pl.program_id(0), pl.program_id(1)
    core = device % 2

    @pl.when((leaf == 0) & (part == 0))
    def _():
        copies = window_copies(pieces, win, sems, core)
        for c in copies:
            c.start()
        for c in copies:
            c.wait()

    @pl.when(part == 0)
    def _():
        ut_ref[...] = u_ref[0].T
        st_ref[...] = s_ref[0].T

    ut = ut_ref[...]
    st = st_ref[...]
    own = 2 * device + leaf
    count = a_ref.shape[1]
    for n in range(count):
        j = nbrs[leaf, part * count + n]
        j = jnp.where(j < 0, own, j)
        half = jnp.dot(ut, a_ref[0, n], preferred_element_type=F32).astype(BF)
        top, bottom = half[:RANK], half[RANK:]
        grown = bottom.astype(F32) - jnp.dot(st, top, preferred_element_type=F32)
        gh, gl = split(grown)
        us = win[window_slot(j, device)]
        both = jnp.dot(jnp.concatenate([gh, gl], 0), us, preferred_element_type=F32)
        p1_ref[0, n] = both[:RANK] + both[RANK:]
        hs_ref[0, n] = bottom


def near_products(leaf_nbrs, bases, shift, near_blocks, pieces):
    sd = jax.ShapeDtypeStruct
    parts = 2
    count = SLOTS // parts
    hbm = pl.BlockSpec(memory_space=pl.ANY)
    return pl.pallas_call(
        near_body,
        grid_spec=pltpu.PrefetchScalarGridSpec(
            num_scalar_prefetch=1,
            grid=(2, parts),
            in_specs=[
                pl.BlockSpec((1, 256, 256), lambda l, p, nb: (l, 0, 0)),
                pl.BlockSpec((1, RANK, RANK), lambda l, p, nb: (l, 0, 0)),
                pl.BlockSpec((1, count, 256, 256), lambda l, p, nb: (l, p, 0, 0)),
            ]
            + [hbm] * 10,
            out_specs=[
                pl.BlockSpec((1, count, RANK, RANK), lambda l, p, nb: (l, p, 0, 0)),
                pl.BlockSpec((1, count, RANK, 256), lambda l, p, nb: (l, p, 0, 0)),
            ],
            scratch_shapes=[
                pltpu.VMEM((256, 256), BF),
                pltpu.VMEM((RANK, RANK), BF),
                pltpu.VMEM((WINDOW, 256, RANK), BF),
                pltpu.SemaphoreType.DMA((10,)),
            ],
        ),
        out_shape=(sd((2, SLOTS, RANK, RANK), F32), sd((2, SLOTS, RANK, 256), BF)),
        compiler_params=pltpu.CompilerParams(vmem_limit_bytes=VMEM),
        name="near_products",
    )(leaf_nbrs, bases, shift, near_blocks, *pieces)


def merge_body(nbrs, pnbrs, p1_ref, hs_ref, sk_ref, *refs):
    pieces = refs[:10]
    out_ref, ex_ref, win, sems = refs[10:]
    device = lax.axis_index("leaf")
    leaf = pl.program_id(0)
    core = device % 2

    @pl.when(leaf == 0)
    def _():
        copies = window_copies(pieces, win, sems, core)
        for c in copies:
            c.start()
        for c in copies:
            c.wait()

    own = 2 * device + leaf
    parent = own // CHILDREN
    out_ref[...] = jnp.zeros_like(out_ref)
    mine = pl.multiple_of((own % CHILDREN) * RANK, RANK)
    for q in range(PNB):

        @pl.when(pnbrs[parent, q] == parent)
        def _():
            out_ref[0, q, :, pl.ds(mine, RANK)] = sk_ref[0]

    for n in range(SLOTS):
        j = nbrs[leaf, n]
        goal = jnp.maximum(j, 0) // CHILDREN
        q = jnp.int32(-1)
        for t in range(PNB):
            q = jnp.where(pnbrs[parent, t] == goal, t, q)

        @pl.when((j >= 0) & (q >= 0))
        def _():
            at = pl.multiple_of((j % CHILDREN) * RANK, RANK)
            d = win[window_slot(j, device)]
            out_ref[0, q, :, pl.ds(at, RANK)] = p1_ref[0, n] - jnp.dot(
                hs_ref[0, n], d, preferred_element_type=F32
            )

    place = device % 4
    for m in range(1, 4):
        at = pl.multiple_of((place ^ m) * 256, 256)
        ex_ref[m - 1] = out_ref[0, 0, :, pl.ds(at, 256)].T.astype(BF)


def merge(leaf_nbrs, parent_nbrs, p1, hs, skeleton, pieces):
    sd = jax.ShapeDtypeStruct
    hbm = pl.BlockSpec(memory_space=pl.ANY)
    return pl.pallas_call(
        merge_body,
        grid_spec=pltpu.PrefetchScalarGridSpec(
            num_scalar_prefetch=2,
            grid=(2,),
            in_specs=[
                pl.BlockSpec((1, SLOTS, RANK, RANK), lambda l, a, b: (l, 0, 0, 0)),
                pl.BlockSpec((1, SLOTS, RANK, 256), lambda l, a, b: (l, 0, 0, 0)),
                pl.BlockSpec((1, RANK, RANK), lambda l, a, b: (l, 0, 0)),
            ]
            + [hbm] * 10,
            out_specs=[
                pl.BlockSpec((1, PNB, RANK, CHILDREN * RANK), lambda l, a, b: (l, 0, 0, 0)),
                pl.BlockSpec((3, 256, RANK), lambda l, a, b: (0, 0, l)),
            ],
            scratch_shapes=[
                pltpu.VMEM((WINDOW, 256, RANK), BF),
                pltpu.SemaphoreType.DMA((10,)),
            ],
        ),
        out_shape=(sd((2, PNB, RANK, CHILDREN * RANK), F32), sd((3, 256, 256), BF)),
        compiler_params=pltpu.CompilerParams(vmem_limit_bytes=VMEM),
        name="merge_rows",
    )(leaf_nbrs, parent_nbrs, p1, hs, skeleton, *pieces)


def symmetric_body(rows_ref, r1_ref, r2_ref, r3_ref, out_ref):
    place = lax.axis_index("leaf") % 4
    rows = [rows_ref[0, 0], rows_ref[1, 0]]
    del rows
    for m, ref in enumerate((None, r1_ref, r2_ref, r3_ref)):
        at = pl.multiple_of((place ^ m) * 256, 256)
        own = jnp.concatenate([rows_ref[l, 0, :, pl.ds(at, 256)] for l in range(2)], 0)
        turned = own.T if m == 0 else ref[...].astype(F32)
        out_ref[:, pl.ds(at, 256)] = 0.5 * (own + turned)


def symmetric(merged, received):
    return pl.pallas_call(
        symmetric_body,
        grid=(1,),
        in_specs=[pl.BlockSpec((2, 1, RANK, CHILDREN * RANK), lambda i: (0, 0, 0, 0))]
        + [pl.BlockSpec((256, 256), lambda i: (0, 0))] * 3,
        out_specs=pl.BlockSpec((256, CHILDREN * RANK), lambda i: (0, 0)),
        out_shape=jax.ShapeDtypeStruct((256, CHILDREN * RANK), F32),
        compiler_params=pltpu.CompilerParams(vmem_limit_bytes=VMEM),
        name="symmetric_rows",
    )(merged, *received)


def swap(value, mask):
    pairs = [(source, source ^ mask) for source in range(lax.axis_size("leaf"))]
    return lax.ppermute(value, "leaf", pairs)


def across(value, apart):
    count = lax.axis_size("leaf")
    pairs = []
    for lower in range(1, count, 2):
        upper = (lower - 1 + 2 * apart) % count
        pairs += [(lower, upper), (upper, lower)]
    return lax.ppermute(value, "leaf", pairs)


def spread(own):
    other = swap(own, 1)
    both = jnp.concatenate([own, other])
    first = across(both, 1)
    third = across(both, 3)
    fourth = across(both, 4)
    first_other = swap(first, 1)
    second = across(first_other, 1)
    return (
        own, other, first, first_other, second, swap(second, 1),
        third, swap(third, 1), fourth, swap(fourth, 1),
    )


def local(near_blocks, diag_blocks, bases, leaf_nbrs, parent_nbrs):
    skeleton_bases = spread(bases[:, :, RANK:])
    leaf_factor, leaf_panel, skeleton, leaf_shift, turned = k0(bases, diag_blocks)
    turned_bases = spread(turned)
    p1, hs = near_products(leaf_nbrs, bases, leaf_shift, near_blocks, skeleton_bases)
    merged, exchange = merge(leaf_nbrs, parent_nbrs, p1, hs, skeleton, turned_bases)
    received = [swap(exchange[m - 1], m) for m in range(1, 4)]
    parent_block = symmetric(merged, received)
    return (leaf_factor, leaf_panel, merged, parent_block)


def solution(mesh):
    in_specs = (
        P("leaf", None, None, None),
        P("leaf", None, None),
        P("leaf", None, None),
        P("leaf", None),
        P(),
    )
    out_specs = (
        P("leaf", None, None),
        P("leaf", None, None),
        P("leaf", None, None, None),
        P("leaf", None),
    )
    return jax.shard_map(local, mesh=mesh, in_specs=in_specs, out_specs=out_specs, check_vma=False)
```

time: 248 us -> 97.6 us (0.39)
  the two profiles are of different devices: /device:TPU:7 before, /device:TPU:1 now
where the time goes in v1:
time: 97.6 us; the launch traced here: 98 us
  starting transfers between devices  38.3 us (39%)
  Pallas kernels  35.1 us (36%)
  waiting for transfers between devices  12.2 us (12%)
  local copies, waits for them, and re-layouts  11.6 us (12%)
    ppermute x13, starting transfers between devices, swap(): return lax.ppermute(value, 'leaf', pairs)  25.7 us
    pallas_call x1, Pallas kernels, near_products(): pl.pallas_call(near_body, grid_spec=pltpu.PrefetchScalarGridSpec(num_scal...  15.6 us
    ppermute x8, starting transfers between devices, across(): return lax.ppermute(value, 'leaf', pairs)  12.6 us
    pallas_call x1, Pallas kernels, merge(): pl.pallas_call(merge_body, grid_spec=pltpu.PrefetchScalarGridSpec(num_sca...  11.9 us
    unnamed x20, local copies, waits for them, and re-layouts  10.6 us
    ppermute x13, waiting for transfers between devices, swap(): return lax.ppermute(value, 'leaf', pairs)  7.91 us
    pallas_call x1, Pallas kernels, k0(): pl.pallas_call(k0_body, out_shape=(sd((2, 128, 128), F32), sd((2, 128, 12...  6.36 us
    ppermute x8, waiting for transfers between devices, across(): return lax.ppermute(value, 'leaf', pairs)  4.3 us
  transfers between devices with their start and end apart: 21, of which 6 were waited for; matrix products, arithmetic and copies ran while one was open for 1% of the time, Pallas kernels for 22%

profile of v1, /device:TPU:1, one launch (start us, length us, event | category | flops | bytes accessed | tf_op | source)
XLA Modules:
  0.0 98.0 jit_solution(14626893160835912491)
XLA Ops:
  0.6 0.9 slice.12.refs_0_
  1.6 3.3 %collective-permute-start = (bf16[2,256,128]{2,1,0:T(8,128)(2,1)S(1)}, bf16[2,256,128]{2,1,0:T(8,128)(2,1)S(1)}, u32[]{:S(2)}, u32[]{:S(2)}) collective-permute-start(bf16[2,256,128]{2,1,0:T(8,128)(2,1)S(1)} %slice.12.refs_0_), channel_id=1, source_target_pairs={{0,1},{1,0},{2,3},{3,2},{4,5},{5,4},{6,7},{7,6},{8,9},{9,8},{10,11... | collective-permute-start | bytes 393224 | tf_op jit(solution)/shard_map/ppermute | solution.py:333
  4.9 0.9 copy-done.2
  5.8 0.9 copy-done.4
  6.8 6.4 %leaf_elimination.1 = (f32[2,128,128]{2,1,0:T(8,128)}, f32[2,128,128]{2,1,0:T(8,128)}, f32[2,128,128]{2,1,0:T(8,128)S(1)}, bf16[2,128,128]{2,1,0:T(8,128)(2,1)S(1)}, bf16[2,256,128]{2,1,0:T(8,128)(2,1)S(1)}) custom-call(bf16[2,256,256]{2,1,0:T(8,128)(2,1)S(1)} %copy-done.2, bf16[2,256,256]{2,1,0:T(8,128)(2,1)S(1)} %copy-done.4), custom_call_target="tpu_custom_call" | custom-call | tf_op jit(solution)/shard_map/leaf_elimination/pallas_call | solution.py:129
  13.1 0.6 copy-done.6
  13.9 1.2 %collective-permute-done.9.refs_1_ = bf16[2,256,128]{2,1,0:T(8,128)(2,1)S(1)} collective-permute-done((bf16[2,256,128]{2,1,0:T(8,128)(2,1)S(1)}, bf16[2,256,128]{2,1,0:T(8,128)(2,1)S(1)}, u32[]{:S(2)}, u32[]{:S(2)}) %collective-permute-start.9) | collective-permute-done | bytes 131104 | tf_op jit(solution)/shard_map/ppermute | solution.py:333
  15.1 0.6 collective-permute-start.10
  15.8 3.9 %collective-permute-done.1.refs_2_ = bf16[4,256,128]{2,1,0:T(8,128)(2,1)S(1)} collective-permute-done((bf16[4,256,128]{2,1,0:T(8,128)(2,1)S(1)}, bf16[4,256,128]{2,1,0:T(8,128)(2,1)S(1)}, u32[]{:S(2)}, u32[]{:S(2)}) %collective-permute-start.1) | collective-permute-done | bytes 262176 | tf_op jit(solution)/shard_map/ppermute | solution.py:342
  19.7 7.1 %collective-permute-start.2 = (bf16[4,256,128]{2,1,0:T(8,128)(2,1)S(1)}, bf16[4,256,128]{2,1,0:T(8,128)(2,1)S(1)}, u32[]{:S(2)}, u32[]{:S(2)}) collective-permute-start(bf16[4,256,128]{2,1,0:T(8,128)(2,1)S(1)} %collective-permute-done.1.refs_2_), channel_id=1, source_target_pairs={{0,1},{1,0},{2,3},{3,2},{4,5},{5,4},{6,7},{7,6},{8,9},{9,8},{10,11... | collective-permute-start | bytes 786440 | tf_op jit(solution)/shard_map/ppermute | solution.py:333
  26.9 7.3 %collective-permute-start.5 = (bf16[4,256,128]{2,1,0:T(8,128)(2,1)S(1)}, bf16[4,256,128]{2,1,0:T(8,128)(2,1)S(1)}, u32[]{:S(2)}, u32[]{:S(2)}) collective-permute-start(bf16[4,256,128]{2,1,0:T(8,128)(2,1)S(1)} %pad_maximum_fusion), channel_id=1, source_target_pairs={{1,6},{6,1},{3,8},{8,3},{5,10},{10,5},{7,12},{12,7},{9,14},{14,9},... | collective-permute-start | bytes 786440 | tf_op jit(solution)/shard_map/ppermute | solution.py:342
  34.2 0.7 collective-permute-start.3
  34.9 3.4 %collective-permute-start.14 = (bf16[4,256,128]{2,1,0:T(8,128)(2,1)S(1)}, bf16[4,256,128]{2,1,0:T(8,128)(2,1)S(1)}, u32[]{:S(2)}, u32[]{:S(2)}) collective-permute-start(bf16[4,256,128]{2,1,0:T(8,128)(2,1)S(1)} %constant_dynamic-update-slice_fusion), channel_id=1, source_target_pairs={{1,6},{6,1},{3,8},{8,3},{5,10},{10,5},{7,12},{12,7},{9,14},{14,9},... | collective-permute-start | bytes 786440 | tf_op jit(solution)/shard_map/ppermute | solution.py:342
  38.4 0.9 collective-permute-start.8
  39.3 0.5 collective-permute-start.12
  39.8 0.2 collective-permute-done.16.refs_8_
  40.0 4.2 %collective-permute-start.6 = (bf16[4,256,128]{2,1,0:T(8,128)(2,1)S(1)}, bf16[4,256,128]{2,1,0:T(8,128)(2,1)}, u32[]{:S(2)}, u32[]{:S(2)}) collective-permute-start(bf16[4,256,128]{2,1,0:T(8,128)(2,1)S(1)} %collective-permute-done.5.refs_6_), channel_id=1, source_target_pairs={{0,1},{1,0},{2,3},{3,2},{4,5},{5,4},{6,7},{7,6},{8,9},{9,8},{10,11... | collective-permute-start | bytes 786440 | tf_op jit(solution)/shard_map/ppermute | solution.py:333
  44.2 2.3 %collective-permute-start.4 = (bf16[4,256,128]{2,1,0:T(8,128)(2,1)S(1)}, bf16[4,256,128]{2,1,0:T(8,128)(2,1)}, u32[]{:S(2)}, u32[]{:S(2)}) collective-permute-start(bf16[4,256,128]{2,1,0:T(8,128)(2,1)S(1)} %collective-permute-done.3.refs_4_), channel_id=1, source_target_pairs={{0,1},{1,0},{2,3},{3,2},{4,5},{5,4},{6,7},{7,6},{8,9},{9,8},{10,11... | collective-permute-start | bytes 786440 | tf_op jit(solution)/shard_map/ppermute | solution.py:333
  46.5 2.7 %collective-permute-start.17 = (bf16[4,256,128]{2,1,0:T(8,128)(2,1)S(1)}, bf16[4,256,128]{2,1,0:T(8,128)(2,1)}, u32[]{:S(2)}, u32[]{:S(2)}) collective-permute-start(bf16[4,256,128]{2,1,0:T(8,128)(2,1)S(1)} %collective-permute-done.16.refs_8_), channel_id=1, source_target_pairs={{0,1},{1,0},{2,3},{3,2},{4,5},{5,4},{6,7},{7,6},{8,9},{9,8},{10,11... | collective-permute-start | bytes 786440 | tf_op jit(solution)/shard_map/ppermute | solution.py:333
  49.2 2.9 %collective-permute-start.13 = (bf16[4,256,128]{2,1,0:T(8,128)(2,1)S(1)}, bf16[4,256,128]{2,1,0:T(8,128)(2,1)}, u32[]{:S(2)}, u32[]{:S(2)}) collective-permute-start(bf16[4,256,128]{2,1,0:T(8,128)(2,1)S(1)} %collective-permute-done.12.refs_4_), channel_id=1, source_target_pairs={{0,1},{1,0},{2,3},{3,2},{4,5},{5,4},{6,7},{7,6},{8,9},{9,8},{10,11... | collective-permute-start | bytes 786440 | tf_op jit(solution)/shard_map/ppermute | solution.py:333
  52.1 1.4 %copy.9.pnbrs = s32[64,5]{1,0:T(8,128)} copy(s32[64,5]{0,1:T(8,128)} %param.9) | data formatting | bytes 2560 | tf_op args[4]
  53.5 0.9 copy-done.3
  54.5 0.8 copy-done.7
  55.3 0.7 copy-done.8
  56.0 15.6 %near_products.1 = (f32[2,26,128,128]{3,2,1,0:T(8,128)S(1)}, bf16[2,26,128,256]{3,2,1,0:T(8,128)(2,1)}) custom-call(s32[2,26]{1,0:T(2,128)S(1)} %copy-done.8, bf16[2,256,256]{2,1,0:T(8,128)(2,1)S(1)} %copy-done.3, bf16[2,128,128]{2,1,0:T(8,128)(2,1)S(1)} %copy-done.7, bf16[2,26,256,256]{3,2,1,0:T(8,128)(2,1)} %a_ref.3, ...), custom_call_target="tpu_custom_call" | custom-call | tf_op jit(solution)/shard_map/near_products/pallas_call | solution.py:204
  71.6 1.8 %copy-done.1 = f32[2,26,128,128]{3,2,1,0:T(8,128)} copy-done((f32[2,26,128,128]{3,2,1,0:T(8,128)}, f32[2,26,128,128]{3,2,1,0:T(8,128)S(1)}, u32[]{:S(2)}) %copy-start.1) | copy-done | bytes 3407896
  73.4 11.9 %merge_rows.1 = (f32[2,5,128,1024]{3,2,1,0:T(8,128)}, bf16[3,256,256]{2,1,0:T(8,128)(2,1)S(1)}) custom-call(s32[2,26]{1,0:T(2,128)S(1)} %copy-done.8, s32[64,5]{1,0:T(8,128)S(1)} %copy-done.5, f32[2,26,128,128]{3,2,1,0:T(8,128)} %copy-done.1, bf16[2,26,128,256]{3,2,1,0:T(8,128)(2,1)} %get-tuple-element.17.hs_ref, ...), custom_call_target="tpu_custom_call" | custom-call | tf_op jit(solution)/shard_map/merge_rows/pallas_call | solution.py:281
  85.4 2.1 %collective-permute-start.19 = (bf16[256,256]{1,0:T(8,128)(2,1)S(1)}, bf16[256,256]{1,0:T(8,128)(2,1)S(1)}, u32[]{:S(2)}, u32[]{:S(2)}) collective-permute-start(bf16[256,256]{1,0:T(8,128)(2,1)S(1)} %get-tuple-element.23), channel_id=1, source_target_pairs={{0,2},{1,3},{2,0},{3,1},{4,6},{5,7},{6,4},{7,5},{8,10},{9,11},{10,... | collective-permute-start | bytes 393224 | tf_op jit(solution)/shard_map/ppermute | solution.py:333
  87.5 3.9 %collective-permute-done.20.r3_ref = bf16[256,256]{1,0:T(8,128)(2,1)S(1)} collective-permute-done((bf16[256,256]{1,0:T(8,128)(2,1)S(1)}, bf16[256,256]{1,0:T(8,128)(2,1)S(1)}, u32[]{:S(2)}, u32[]{:S(2)}) %collective-permute-start.20) | collective-permute-done | bytes 131104 | tf_op jit(solution)/shard_map/ppermute | solution.py:333
  91.4 2.8 %collective-permute-done.19.r2_ref = bf16[256,256]{1,0:T(8,128)(2,1)S(1)} collective-permute-done((bf16[256,256]{1,0:T(8,128)(2,1)S(1)}, bf16[256,256]{1,0:T(8,128)(2,1)S(1)}, u32[]{:S(2)}, u32[]{:S(2)}) %collective-permute-start.19) | collective-permute-done | bytes 131104 | tf_op jit(solution)/shard_map/ppermute | solution.py:333
  94.2 2.5 %copy-done = f32[2,5,128,1024]{3,2,1,0:T(8,128)S(1)} copy-done((f32[2,5,128,1024]{3,2,1,0:T(8,128)S(1)}, f32[2,5,128,1024]{3,2,1,0:T(8,128)}, u32[]{:S(2)}) %copy-start) | copy-done | bytes 5242904
  96.7 1.3 %symmetric_rows.1 = f32[256,1024]{1,0:T(8,128)} custom-call(f32[2,5,128,1024]{3,2,1,0:T(8,128)S(1)} %copy-done, bf16[256,256]{1,0:T(8,128)(2,1)S(1)} %collective-permute-done.18.r1_ref, bf16[256,256]{1,0:T(8,128)(2,1)S(1)} %collective-permute-done.19.r2_ref, bf16[256,256]{1,0:T(8,128)(2,1)S(1)} %collective-permute-done.20.r3_ref), custom_call_target="tpu_custom_call" | custom-call | tf_op jit(solution)/shard_map/symmetric_rows/pallas_call | solution.py:319
  (38 shorter events, 0.5 us)
Async XLA Ops:
  1.6 12.3 %collective-permute-start = (bf16[2,256,128]{2,1,0:T(8,128)(2,1)S(1)}, bf16[2,256,128]{2,1,0:T(8,128)(2,1)S(1)}, u32[]{:S(2)}, u32[]{:S(2)}) collective-permute-start(bf16[2,256,128]{2,1,0:T(8,128)(2,1)S(1)} %slice.12.refs_0_), channel_id=1, source_target_pairs={{0,1},{1,0},{2,3},{3,2},{4,5},{5,4},{6,7},{7,6},{8,9},{9,8},{10,11... | collective-permute-start | bytes 393224 | tf_op jit(solution)/shard_map/ppermute | solution.py:333
  4.9 0.9 copy-start.2
  5.8 0.9 copy-start.4
  13.1 0.6 copy-start.6
  13.8 1.3 %collective-permute-start.9 = (bf16[2,256,128]{2,1,0:T(8,128)(2,1)S(1)}, bf16[2,256,128]{2,1,0:T(8,128)(2,1)S(1)}, u32[]{:S(2)}, u32[]{:S(2)}) collective-permute-start(bf16[2,256,128]{2,1,0:T(8,128)(2,1)S(1)} %get-tuple-element.19.refs_0_), channel_id=1, source_target_pairs={{0,1},{1,0},{2,3},{3,2},{4,5},{5,4},{6,7},{7,6},{8,9},{9,8},{10,11... | collective-permute-start | bytes 393224 | tf_op jit(solution)/shard_map/ppermute | solution.py:333
  13.8 5.9 %collective-permute-start.1 = (bf16[4,256,128]{2,1,0:T(8,128)(2,1)S(1)}, bf16[4,256,128]{2,1,0:T(8,128)(2,1)S(1)}, u32[]{:S(2)}, u32[]{:S(2)}) collective-permute-start(bf16[4,256,128]{2,1,0:T(8,128)(2,1)S(1)} %pad_maximum_fusion), channel_id=1, source_target_pairs={{1,2},{2,1},{3,4},{4,3},{5,6},{6,5},{7,8},{8,7},{9,10},{10,9},{11,... | collective-permute-start | bytes 786440 | tf_op jit(solution)/shard_map/ppermute | solution.py:342
  15.1 19.1 %collective-permute-start.10 = (bf16[4,256,128]{2,1,0:T(8,128)(2,1)S(1)}, bf16[4,256,128]{2,1,0:T(8,128)(2,1)S(1)}, u32[]{:S(2)}, u32[]{:S(2)}) collective-permute-start(bf16[4,256,128]{2,1,0:T(8,128)(2,1)S(1)} %constant_dynamic-update-slice_fusion), channel_id=1, source_target_pairs={{1,2},{2,1},{3,4},{4,3},{5,6},{6,5},{7,8},{8,7},{9,10},{10,9},{11,... | collective-permute-start | bytes 786440 | tf_op jit(solution)/shard_map/ppermute | solution.py:342
  19.7 14.5 %collective-permute-start.2 = (bf16[4,256,128]{2,1,0:T(8,128)(2,1)S(1)}, bf16[4,256,128]{2,1,0:T(8,128)(2,1)S(1)}, u32[]{:S(2)}, u32[]{:S(2)}) collective-permute-start(bf16[4,256,128]{2,1,0:T(8,128)(2,1)S(1)} %collective-permute-done.1.refs_2_), channel_id=1, source_target_pairs={{0,1},{1,0},{2,3},{3,2},{4,5},{5,4},{6,7},{7,6},{8,9},{9,8},{10,11... | collective-permute-start | bytes 786440 | tf_op jit(solution)/shard_map/ppermute | solution.py:333
  26.9 8.0 %collective-permute-start.7 = (bf16[4,256,128]{2,1,0:T(8,128)(2,1)S(1)}, bf16[4,256,128]{2,1,0:T(8,128)(2,1)S(1)}, u32[]{:S(2)}, u32[]{:S(2)}) collective-permute-start(bf16[4,256,128]{2,1,0:T(8,128)(2,1)S(1)} %pad_maximum_fusion), channel_id=1, source_target_pairs={{1,8},{8,1},{3,10},{10,3},{5,12},{12,5},{7,14},{14,7},{9,16},{16,9... | collective-permute-start | bytes 786440 | tf_op jit(solution)/shard_map/ppermute | solution.py:342
  26.9 11.5 %collective-permute-start.5 = (bf16[4,256,128]{2,1,0:T(8,128)(2,1)S(1)}, bf16[4,256,128]{2,1,0:T(8,128)(2,1)S(1)}, u32[]{:S(2)}, u32[]{:S(2)}) collective-permute-start(bf16[4,256,128]{2,1,0:T(8,128)(2,1)S(1)} %pad_maximum_fusion), channel_id=1, source_target_pairs={{1,6},{6,1},{3,8},{8,3},{5,10},{10,5},{7,12},{12,7},{9,14},{14,9},... | collective-permute-start | bytes 786440 | tf_op jit(solution)/shard_map/ppermute | solution.py:342
  34.2 5.1 %collective-permute-start.11 = (bf16[4,256,128]{2,1,0:T(8,128)(2,1)S(1)}, bf16[4,256,128]{2,1,0:T(8,128)(2,1)S(1)}, u32[]{:S(2)}, u32[]{:S(2)}) collective-permute-start(bf16[4,256,128]{2,1,0:T(8,128)(2,1)S(1)} %collective-permute-done.10.refs_2_), channel_id=1, source_target_pairs={{0,1},{1,0},{2,3},{3,2},{4,5},{5,4},{6,7},{7,6},{8,9},{9,8},{10,11... | collective-permute-start | bytes 786440 | tf_op jit(solution)/shard_map/ppermute | solution.py:333
  34.2 5.8 %collective-permute-start.16 = (bf16[4,256,128]{2,1,0:T(8,128)(2,1)S(1)}, bf16[4,256,128]{2,1,0:T(8,128)(2,1)S(1)}, u32[]{:S(2)}, u32[]{:S(2)}) collective-permute-start(bf16[4,256,128]{2,1,0:T(8,128)(2,1)S(1)} %constant_dynamic-update-slice_fusion), channel_id=1, source_target_pairs={{1,8},{8,1},{3,10},{10,3},{5,12},{12,5},{7,14},{14,7},{9,16},{16,9... | collective-permute-start | bytes 786440 | tf_op jit(solution)/shard_map/ppermute | solution.py:342
  34.2 9.9 %collective-permute-start.3 = (bf16[4,256,128]{2,1,0:T(8,128)(2,1)S(1)}, bf16[4,256,128]{2,1,0:T(8,128)(2,1)S(1)}, u32[]{:S(2)}, u32[]{:S(2)}) collective-permute-start(bf16[4,256,128]{2,1,0:T(8,128)(2,1)S(1)} %collective-permute-done.2.refs_3_), channel_id=1, source_target_pairs={{1,2},{2,1},{3,4},{4,3},{5,6},{6,5},{7,8},{8,7},{9,10},{10,9},{11,... | collective-permute-start | bytes 786440 | tf_op jit(solution)/shard_map/ppermute | solution.py:342
  34.9 11.6 %collective-permute-start.14 = (bf16[4,256,128]{2,1,0:T(8,128)(2,1)S(1)}, bf16[4,256,128]{2,1,0:T(8,128)(2,1)S(1)}, u32[]{:S(2)}, u32[]{:S(2)}) collective-permute-start(bf16[4,256,128]{2,1,0:T(8,128)(2,1)S(1)} %constant_dynamic-update-slice_fusion), channel_id=1, source_target_pairs={{1,6},{6,1},{3,8},{8,3},{5,10},{10,5},{7,12},{12,7},{9,14},{14,9},... | collective-permute-start | bytes 786440 | tf_op jit(solution)/shard_map/ppermute | solution.py:342
  38.4 10.9 %collective-permute-start.8 = (bf16[4,256,128]{2,1,0:T(8,128)(2,1)S(1)}, bf16[4,256,128]{2,1,0:T(8,128)(2,1)S(1)}, u32[]{:S(2)}, u32[]{:S(2)}) collective-permute-start(bf16[4,256,128]{2,1,0:T(8,128)(2,1)S(1)} %collective-permute-done.7.refs_8_), channel_id=1, source_target_pairs={{0,1},{1,0},{2,3},{3,2},{4,5},{5,4},{6,7},{7,6},{8,9},{9,8},{10,11... | collective-permute-start | bytes 786440 | tf_op jit(solution)/shard_map/ppermute | solution.py:333
  39.3 9.9 %collective-permute-start.12 = (bf16[4,256,128]{2,1,0:T(8,128)(2,1)S(1)}, bf16[4,256,128]{2,1,0:T(8,128)(2,1)S(1)}, u32[]{:S(2)}, u32[]{:S(2)}) collective-permute-start(bf16[4,256,128]{2,1,0:T(8,128)(2,1)S(1)} %collective-permute-done.11.refs_3_), channel_id=1, source_target_pairs={{1,2},{2,1},{3,4},{4,3},{5,6},{6,5},{7,8},{8,7},{9,10},{10,9},{11,... | collective-permute-start | bytes 786440 | tf_op jit(solution)/shard_map/ppermute | solution.py:342
  40.0 13.5 %collective-permute-start.6 = (bf16[4,256,128]{2,1,0:T(8,128)(2,1)S(1)}, bf16[4,256,128]{2,1,0:T(8,128)(2,1)}, u32[]{:S(2)}, u32[]{:S(2)}) collective-permute-start(bf16[4,256,128]{2,1,0:T(8,128)(2,1)S(1)} %collective-permute-done.5.refs_6_), channel_id=1, source_target_pairs={{0,1},{1,0},{2,3},{3,2},{4,5},{5,4},{6,7},{7,6},{8,9},{9,8},{10,11... | collective-permute-start | bytes 786440 | tf_op jit(solution)/shard_map/ppermute | solution.py:333
  44.2 9.4 %collective-permute-start.4 = (bf16[4,256,128]{2,1,0:T(8,128)(2,1)S(1)}, bf16[4,256,128]{2,1,0:T(8,128)(2,1)}, u32[]{:S(2)}, u32[]{:S(2)}) collective-permute-start(bf16[4,256,128]{2,1,0:T(8,128)(2,1)S(1)} %collective-permute-done.3.refs_4_), channel_id=1, source_target_pairs={{0,1},{1,0},{2,3},{3,2},{4,5},{5,4},{6,7},{7,6},{8,9},{9,8},{10,11... | collective-permute-start | bytes 786440 | tf_op jit(solution)/shard_map/ppermute | solution.py:333
  46.5 26.8 %collective-permute-start.17 = (bf16[4,256,128]{2,1,0:T(8,128)(2,1)S(1)}, bf16[4,256,128]{2,1,0:T(8,128)(2,1)}, u32[]{:S(2)}, u32[]{:S(2)}) collective-permute-start(bf16[4,256,128]{2,1,0:T(8,128)(2,1)S(1)} %collective-permute-done.16.refs_8_), channel_id=1, source_target_pairs={{0,1},{1,0},{2,3},{3,2},{4,5},{5,4},{6,7},{7,6},{8,9},{9,8},{10,11... | collective-permute-start | bytes 786440 | tf_op jit(solution)/shard_map/ppermute | solution.py:333
  49.2 24.1 %collective-permute-start.15 = (bf16[4,256,128]{2,1,0:T(8,128)(2,1)S(1)}, bf16[4,256,128]{2,1,0:T(8,128)(2,1)}, u32[]{:S(2)}, u32[]{:S(2)}) collective-permute-start(bf16[4,256,128]{2,1,0:T(8,128)(2,1)S(1)} %collective-permute-done.14.refs_6_), channel_id=1, source_target_pairs={{0,1},{1,0},{2,3},{3,2},{4,5},{5,4},{6,7},{7,6},{8,9},{9,8},{10,11... | collective-permute-start | bytes 786440 | tf_op jit(solution)/shard_map/ppermute | solution.py:333
  49.2 24.1 %collective-permute-start.13 = (bf16[4,256,128]{2,1,0:T(8,128)(2,1)S(1)}, bf16[4,256,128]{2,1,0:T(8,128)(2,1)}, u32[]{:S(2)}, u32[]{:S(2)}) collective-permute-start(bf16[4,256,128]{2,1,0:T(8,128)(2,1)S(1)} %collective-permute-done.12.refs_4_), channel_id=1, source_target_pairs={{0,1},{1,0},{2,3},{3,2},{4,5},{5,4},{6,7},{7,6},{8,9},{9,8},{10,11... | collective-permute-start | bytes 786440 | tf_op jit(solution)/shard_map/ppermute | solution.py:333
  53.5 1.0 copy-start.3
  54.5 0.8 copy-start.7
  55.3 0.7 copy-start.8
  56.0 17.4 %copy-start.5 = (s32[64,5]{1,0:T(8,128)S(1)}, s32[64,5]{1,0:T(8,128)}, u32[]{:S(2)}) copy-start(s32[64,5]{1,0:T(8,128)} %copy.9.pnbrs) | copy-start | bytes 3844
  71.6 1.8 %copy-start.1 = (f32[2,26,128,128]{3,2,1,0:T(8,128)}, f32[2,26,128,128]{3,2,1,0:T(8,128)S(1)}, u32[]{:S(2)}) copy-start(f32[2,26,128,128]{3,2,1,0:T(8,128)S(1)} %get-tuple-element.16.p1_ref) | copy-start | bytes 10223620
  85.3 6.1 %collective-permute-start.20 = (bf16[256,256]{1,0:T(8,128)(2,1)S(1)}, bf16[256,256]{1,0:T(8,128)(2,1)S(1)}, u32[]{:S(2)}, u32[]{:S(2)}) collective-permute-start(bf16[256,256]{1,0:T(8,128)(2,1)S(1)} %get-tuple-element.22), channel_id=1, source_target_pairs={{0,3},{1,2},{2,1},{3,0},{4,7},{5,6},{6,5},{7,4},{8,11},{9,10},{10,... | collective-permute-start | bytes 393224 | tf_op jit(solution)/shard_map/ppermute | solution.py:333
  85.4 8.8 %collective-permute-start.19 = (bf16[256,256]{1,0:T(8,128)(2,1)S(1)}, bf16[256,256]{1,0:T(8,128)(2,1)S(1)}, u32[]{:S(2)}, u32[]{:S(2)}) collective-permute-start(bf16[256,256]{1,0:T(8,128)(2,1)S(1)} %get-tuple-element.23), channel_id=1, source_target_pairs={{0,2},{1,3},{2,0},{3,1},{4,6},{5,7},{6,4},{7,5},{8,10},{9,11},{10,... | collective-permute-start | bytes 393224 | tf_op jit(solution)/shard_map/ppermute | solution.py:333
  87.5 6.8 %collective-permute-start.18 = (bf16[256,256]{1,0:T(8,128)(2,1)S(1)}, bf16[256,256]{1,0:T(8,128)(2,1)S(1)}, u32[]{:S(2)}, u32[]{:S(2)}) collective-permute-start(bf16[256,256]{1,0:T(8,128)(2,1)S(1)} %get-tuple-element.24), channel_id=1, source_target_pairs={{0,1},{1,0},{2,3},{3,2},{4,5},{5,4},{6,7},{7,6},{8,9},{9,8},{10,11... | collective-permute-start | bytes 393224 | tf_op jit(solution)/shard_map/ppermute | solution.py:333
  94.2 2.5 %copy-start = (f32[2,5,128,1024]{3,2,1,0:T(8,128)S(1)}, f32[2,5,128,1024]{3,2,1,0:T(8,128)}, u32[]{:S(2)}) copy-start(f32[2,5,128,1024]{3,2,1,0:T(8,128)} %get-tuple-element.11.rows_ref) | copy-start | bytes 15728644

commit v2 on v1

v2 whole, which is shorter than its diff:
```python
import jax
import jax.numpy as jnp
from jax import lax
from jax.experimental import pallas as pl
from jax.experimental.pallas import tpu as pltpu
from jax.sharding import PartitionSpec as P

RANK = 128
REACH = 16
CHILDREN = 8
SLOTS = 26
PNB = 5
REACH_CHIPS = 4
WINDOW = 36
GROUP = 6 + 7
RATE = 1.1e15
VMEM = 24 * 1024 * 1024


F32 = jnp.float32
BF = jnp.bfloat16

def split(x):
    hi = x.astype(BF)
    lo = (x - hi.astype(F32)).astype(BF)
    return hi, lo

def dot00(a, b):
    return lax.dot_general(a, b, (((0,), (0,)), ((), ())), preferred_element_type=F32)

def dot00_3(a, b):
    ah, al = split(a); bh, bl = split(b)
    return dot00(jnp.concatenate([ah, ah, al], 0), jnp.concatenate([bh, bl, bh], 0))

def bc(x):
    return jnp.broadcast_to(x, (8, 128))

def eliminate(blocks, out):
    sub = lax.broadcasted_iota(jnp.int32, (8, 128), 0)
    count = len(blocks)
    done = []
    for k in range(count):
        yield
        parts = blocks[k]
        left = parts[0]
        cols = [bc(left[:, 8*k+j:8*k+j+1]) for j in range(8)]
        s = [[bc(cols[j][i:i+1, :]) for j in range(i+1)] for i in range(8)]
        r = [None]*8
        L = [[None]*8 for _ in range(8)]
        for j in range(8):
            r[j] = lax.rsqrt(s[j][j])
            for i in range(j+1, 8):
                L[i][j] = s[i][j]*r[j]
            for i in range(j+1, 8):
                for m in range(j+1, i+1):
                    s[i][m] = s[i][m] - L[i][j]*L[m][j]
        rows = []
        for j in range(8):
            row = []
            for q, part in enumerate(parts):
                x = bc(part[j:j+1, :])
                for m in range(j):
                    x = x - L[j][m]*rows[m][q]
                row.append(x*r[j])
            rows.append(row)
        packed = []
        for q in range(len(parts)):
            x = rows[0][q]
            for j in range(1, 8):
                x = jnp.where(sub == j, rows[j][q], x)
            packed.append(x)
        done.append(packed)
        if k + 1 < count:
            nxt = blocks[k+1]
            cb = [bc(nxt[0][:, 8*k+j:8*k+j+1]) for j in range(8)]
            lc = []
            new = list(nxt)
            for j in range(8):
                x = cb[j]
                for m in range(j):
                    x = x - lc[m]*L[j][m]
                x = x*r[j]
                lc.append(x)
                new = [new[q] - x*rows[j][q] for q in range(len(new))]
            blocks[k+1] = new
        if k + 2 < count:
            wide = jnp.concatenate(packed, 1)
            upd = dot00_3(packed[0], wide)
            for ib in range(k+2, count):
                blocks[ib] = [blocks[ib][q] - upd[8*ib:8*ib+8, 128*q:128*q+128] for q in range(len(packed))]
    out.extend(done)

def cost(microseconds):
    return pl.CostEstimate(flops=int(microseconds * 1e-6 * RATE), bytes_accessed=0, transcendentals=0)


def k0_body(u_hbm, a_hbm, f_ref, p_ref, sk_ref, s_ref, d_ref, u_ref, a_ref, sems):
    loads = [
        pltpu.make_async_copy(u_hbm, u_ref, sems.at[0]),
        pltpu.make_async_copy(a_hbm, a_ref, sems.at[1]),
    ]
    for load in loads:
        load.start()
    for load in loads:
        load.wait()
    row = lax.broadcasted_iota(jnp.int32, (128, 128), 0)
    col = lax.broadcasted_iota(jnp.int32, (128, 128), 1)
    eye = jnp.where(row == col, 1.0, 0.0).astype(F32)
    outs = []; gens = []
    prep = []
    for l in range(2):
        u = u_ref[l]
        half = dot00(u, a_ref[l]).astype(BF)
        dense = jnp.dot(half, u, preferred_element_type=F32)
        arr = dense[:128, :128]
        arr = 0.5*(arr + arr.T)
        prep.append((u, dense, arr))
    for l in range(2):
        u, dense, arr = prep[l]
        rs = dense[:128, 128:]
        blocks = [[arr[8*i:8*i+8], rs[8*i:8*i+8], eye[8*i:8*i+8]] for i in range(16)]
        outs.append([])
        gens.append(eliminate(blocks, outs[-1]))
    for _ in range(17):
        for g in gens:
            next(g, None)
    for l in range(2):
        u, dense, arr = prep[l]
        done = outs[l]
        upper = jnp.concatenate([d[0] for d in done], 0)
        upper = jnp.where(row <= col, upper, 0.0)
        panel = jnp.concatenate([d[1] for d in done], 0)
        inv = jnp.concatenate([d[2] for d in done], 0)
        f_ref[l] = upper.T
        p_ref[l] = panel
        shift = dot00_3(inv, panel).astype(BF)
        s_ref[l] = shift
        turned = jnp.dot(u[:, :128], shift, preferred_element_type=F32).astype(BF)
        d_ref[l] = jnp.concatenate([u[:, 128:], turned], 1)
        sk_ref[l] = dense[128:, 128:] - dot00_3(panel, panel)

def k0(bases, diag):
    sd = jax.ShapeDtypeStruct
    return pl.pallas_call(
        k0_body,
        in_specs=[pl.BlockSpec(memory_space=pltpu.HBM)] * 2,
        scratch_shapes=[
            pltpu.VMEM((2, 256, 256), BF),
            pltpu.VMEM((2, 256, 256), BF),
            pltpu.SemaphoreType.DMA((2,)),
        ],
        out_shape=(sd((2,128,128),F32), sd((2,128,128),F32), sd((2,128,128),F32), sd((2,128,128),BF), sd((2,256,256),BF)),
        compiler_params=pltpu.CompilerParams(vmem_limit_bytes=VMEM),
        cost_estimate=cost(6.5),
        name="leaf_elimination",
    )(bases, diag)


def slot_table(nbrs, table, device):
    for leaf in range(2):
        for w in range(WINDOW):
            table[leaf, w] = -1
        for n in range(SLOTS):
            j = nbrs[leaf, n]

            @pl.when(j >= 0)
            def _():
                table[leaf, j - 4 * (device // 2) + REACH] = n


def package_leaves(name, device):
    core = device % 2
    kind, k = name
    if kind == "own":
        return [16 + 2 * core + i for i in range(2)]
    if kind == "other":
        return [18 - 2 * core + i for i in range(2)]
    below = (core == 0) if kind == "near" else (core == 1)
    low, high = 4 * (4 - k), 4 * (4 + k)
    if k == 3:
        place = device // 2 % 4
        holder = core if kind == "near" else 1 - core
        end = jnp.where(holder == 0, place == 0, place == 3)
        turned = jnp.where((holder == 1) != end, 2, 0)
        return [jnp.where(holder == 0, high, low) + (i ^ turned) for i in range(4)]
    return [jnp.where(below, low + (i ^ 2), high + i) for i in range(4)]


def near_blocks_of(names, refs, h_ref, s_ref, table, device, put, group=8):
    work = []
    for leaf in range(2):
        index = 0
        for name, ref in zip(names, refs):
            for i, place in enumerate(package_leaves(name, device)):
                if not (name[0] == "own" and i == leaf):
                    work.append((leaf, index, place, ref, i))
                index += 1
    shifts = [s_ref[leaf].T for leaf in range(2)]
    for first in range(0, len(work), group):
        some = work[first : first + group]
        slots = [table[leaf, place] for leaf, _, place, _, _ in some]
        boths = [
            jnp.dot(h_ref[item[0], jnp.maximum(n, 0)], item[3][item[4]], preferred_element_type=F32)
            for item, n in zip(some, slots)
        ]
        rests = []
        for item, both in zip(some, boths):
            hi, lo = split(both[:RANK, :RANK])
            rests.append(jnp.dot(shifts[item[0]], jnp.concatenate([hi, lo], 1), preferred_element_type=F32))
        for (leaf, index, place, _, _), n, both, rest in zip(some, slots, boths, rests):
            block = both[RANK:, :RANK] - both[RANK:, RANK:] - rest[:, :RANK] - rest[:, RANK:]
            put(leaf, index, place, n, block)


def row_of(pnbrs, parent, goal, live, missing):
    q = jnp.int32(missing)
    for t in range(PNB):
        q = jnp.where((pnbrs[t, parent] == goal) & live, t, q)
    return q


def half_body(u_ref, a_ref, h_ref):
    for leaf in range(2):
        ut = u_ref[leaf].T
        for n in range(SLOTS):
            h_ref[leaf, n] = jnp.dot(ut, a_ref[leaf, n], preferred_element_type=F32).astype(BF)


def half_products(bases, near_blocks):
    vmem = pl.BlockSpec(memory_space=pltpu.VMEM)
    return pl.pallas_call(
        half_body,
        in_specs=[vmem, vmem],
        out_specs=vmem,
        out_shape=jax.ShapeDtypeStruct((2, SLOTS, 256, 256), BF),
        compiler_params=pltpu.CompilerParams(vmem_limit_bytes=VMEM),
        cost_estimate=cost(3.5),
        name="half_products",
    )(bases, near_blocks)


INNER = (("own", 0), ("other", 0), ("near", 1), ("far", 1), ("near", 4), ("far", 4))
LAST = (("near", 2), ("far", 2), ("near", 3), ("far", 3))


def inner_body(nbrs, s_ref, h_ref, sk_ref, *refs):
    pieces = refs[:6]
    rows_ref, ex_ref, part_ref, table = refs[6:]
    device = lax.axis_index("leaf")
    slot_table(nbrs, table, device)
    parent = device // 4
    rows_ref[...] = jnp.zeros_like(rows_ref)

    def put(leaf, index, place, n, block):
        j = place + 4 * (device // 2) - REACH
        part_ref[leaf, index] = block
        inside = (n >= 0) & (j // CHILDREN == parent)
        at = pl.multiple_of(jnp.where(inside, j % CHILDREN, CHILDREN) * RANK, RANK)
        rows_ref[leaf, :, pl.ds(at, RANK)] = block

    near_blocks_of(INNER, pieces, h_ref, s_ref, table, device, put)
    for leaf in range(2):
        mine = pl.multiple_of(((2 * device + leaf) % CHILDREN) * RANK, RANK)
        rows_ref[leaf, :, pl.ds(mine, RANK)] = sk_ref[leaf]
        part_ref[leaf, leaf] = sk_ref[leaf]
    place = device % 4
    for m in range(1, 4):
        at = pl.multiple_of((place ^ m) * 256, 256)
        block = jnp.concatenate([rows_ref[leaf, :, pl.ds(at, 256)] for leaf in range(2)], 0)
        ex_ref[m - 1] = block.T.astype(BF)


def inner(leaf_nbrs, shift, halves, skeleton, pieces):
    sd = jax.ShapeDtypeStruct
    vmem = pl.BlockSpec(memory_space=pltpu.VMEM)
    return pl.pallas_call(
        inner_body,
        in_specs=[pl.BlockSpec(memory_space=pltpu.SMEM)] + [vmem] * 9,
        out_specs=[vmem, vmem, vmem],
        scratch_shapes=[pltpu.SMEM((2, WINDOW), jnp.int32)],
        out_shape=(
            sd((2, RANK, (CHILDREN + 1) * RANK), F32),
            sd((3, 256, 256), BF),
            sd((2, 20, RANK, RANK), F32),
        ),
        compiler_params=pltpu.CompilerParams(vmem_limit_bytes=VMEM),
        cost_estimate=cost(0.01),
        name="inner_rows",
    )(leaf_nbrs, shift, halves, skeleton, *pieces)


def outer_body(nbrs, pnbrs, part_ref, out_ref, full, table, sems):
    device = lax.axis_index("leaf")
    slot_table(nbrs, table, device)
    parent = device // 4
    full[...] = jnp.zeros_like(full)
    copies = [
        pltpu.make_async_copy(full.at[leaf, pl.ds(0, PNB)], out_ref.at[leaf], sems.at[leaf]) for leaf in range(2)
    ]
    for leaf in range(2):
        index = 0
        for name in INNER:
            for i, place in enumerate(package_leaves(name, device)):
                mine = name[0] == "own" and i == leaf
                live = True if mine else table[leaf, place] >= 0
                j = place + 4 * (device // 2) - REACH
                q = row_of(pnbrs, parent, j // CHILDREN, live, PNB)
                at = pl.multiple_of((j % CHILDREN) * RANK, RANK)
                full[leaf, q, :, pl.ds(at, RANK)] = part_ref[leaf, index]
                index += 1
        copies[leaf].start()
    for c in copies:
        c.wait()


def outer(leaf_nbrs, parent_nbrs, part):
    return pl.pallas_call(
        outer_body,
        in_specs=[pl.BlockSpec(memory_space=pltpu.SMEM)] * 2 + [pl.BlockSpec(memory_space=pltpu.VMEM)],
        out_specs=pl.BlockSpec(memory_space=pl.ANY),
        scratch_shapes=[
            pltpu.VMEM((2, PNB + 1, RANK, CHILDREN * RANK), F32),
            pltpu.SMEM((2, WINDOW), jnp.int32),
            pltpu.SemaphoreType.DMA((2,)),
        ],
        out_shape=jax.ShapeDtypeStruct((2, PNB, RANK, CHILDREN * RANK), F32),
        compiler_params=pltpu.CompilerParams(vmem_limit_bytes=VMEM),
        cost_estimate=cost(0.01),
        name="outer_rows",
    )(leaf_nbrs, parent_nbrs, part)


def last_body(nbrs, pnbrs, s_ref, h_ref, rows_ref, r1_ref, r2_ref, r3_ref, *refs):
    pieces = refs[:4]
    _, out_ref, block_ref, part, table, sems = refs[4:]
    device = lax.axis_index("leaf")
    slot_table(nbrs, table, device)
    parent = device // 4
    copies = []

    def put(leaf, index, place, n, block):
        j = place + 4 * (device // 2) - REACH
        part[leaf, index] = block
        q = row_of(pnbrs, parent, j // CHILDREN, n >= 0, -1)
        at = pl.multiple_of((j % CHILDREN) * RANK, RANK)
        copy = pltpu.make_async_copy(
            part.at[leaf, index],
            out_ref.at[leaf, jnp.maximum(q, 0), :, pl.ds(at, RANK)],
            sems.at[leaf, index],
        )
        copies.append((q, copy))

        @pl.when(q >= 0)
        def _():
            copy.start()

    near_blocks_of(LAST, pieces, h_ref, s_ref, table, device, put)
    place = device % 4
    for m, ref in enumerate((None, r1_ref, r2_ref, r3_ref)):
        at = pl.multiple_of((place ^ m) * 256, 256)
        own = jnp.concatenate([rows_ref[leaf, :, pl.ds(at, 256)] for leaf in range(2)], 0)
        turned = own.T if m == 0 else ref[...].astype(F32)
        block_ref[:, pl.ds(at, 256)] = 0.5 * (own + turned)
    for q, copy in copies:

        @pl.when(q >= 0)
        def _():
            copy.wait()


def last(leaf_nbrs, parent_nbrs, shift, halves, rows, received, pieces, merged):
    sd = jax.ShapeDtypeStruct
    vmem = pl.BlockSpec(memory_space=pltpu.VMEM)
    hbm = pl.BlockSpec(memory_space=pl.ANY)
    return pl.pallas_call(
        last_body,
        in_specs=[pl.BlockSpec(memory_space=pltpu.SMEM)] * 2 + [vmem] * 10 + [hbm],
        out_specs=[hbm, vmem],
        scratch_shapes=[
            pltpu.VMEM((2, 16, RANK, RANK), F32),
            pltpu.SMEM((2, WINDOW), jnp.int32),
            pltpu.SemaphoreType.DMA((2, 16)),
        ],
        out_shape=(sd((2, PNB, RANK, CHILDREN * RANK), F32), sd((256, CHILDREN * RANK), F32)),
        input_output_aliases={12: 0},
        compiler_params=pltpu.CompilerParams(vmem_limit_bytes=VMEM),
        cost_estimate=cost(0.01),
        name="last_rows",
    )(leaf_nbrs, parent_nbrs, shift, halves, rows, *received, *pieces, merged)


def ring_body(own_ref, far_ref, out_ref, sem):
    device = lax.axis_index("leaf")
    place = device // 2 % 4
    end = jnp.where(device % 2 == 0, place == 0, place == 3)

    @pl.when(end)
    def _():
        copy = pltpu.make_async_copy(own_ref, out_ref, sem)
        copy.start()
        copy.wait()

    @pl.when(jnp.logical_not(end))
    def _():
        copy = pltpu.make_async_copy(far_ref, out_ref, sem)
        copy.start()
        copy.wait()


def ring_package(own, far):
    return pl.pallas_call(
        ring_body,
        in_specs=[pl.BlockSpec(memory_space=pl.ANY)] * 2,
        out_specs=pl.BlockSpec(memory_space=pl.ANY),
        scratch_shapes=[pltpu.SemaphoreType.DMA],
        out_shape=jax.ShapeDtypeStruct(own.shape, own.dtype),
        compiler_params=pltpu.CompilerParams(vmem_limit_bytes=1024 * 1024),
        cost_estimate=cost(0.01),
        name="ring_package",
    )(own, far)


def swap(value, mask):
    pairs = [(source, source ^ mask) for source in range(lax.axis_size("leaf"))]
    return lax.ppermute(value, "leaf", pairs)


def across(value, apart):
    count = lax.axis_size("leaf")
    pairs = count // 2
    matched = [(2 * c + 1, 2 * (c + apart)) for c in range(pairs - apart)]
    low = [2 * c for c in range(min(apart, pairs))]
    high = [2 * c + 1 for c in range(max(pairs - apart, 0), pairs)]
    while len(low) > 1:
        matched += [(low.pop(), low.pop()), (high.pop(), high.pop())]
    if low:
        matched.append((low.pop(), high.pop()))
    return lax.ppermute(value, "leaf", matched + [(b, a) for a, b in matched])


def around(value):
    matched = []
    for lower in range(1, lax.axis_size("leaf"), 2):
        ring, place = divmod(lower // 2, 4)
        matched.append((lower, 2 * (4 * ring + (place + 1) % 4)))
    return lax.ppermute(value, "leaf", matched + [(b, a) for a, b in matched])


def local(near_blocks, diag_blocks, bases, leaf_nbrs, parent_nbrs):
    barrier = lax.optimization_barrier
    leaf_factor, leaf_panel, skeleton, shift, own = k0(
        pltpu.with_memory_space_constraint(bases, pltpu.HBM),
        pltpu.with_memory_space_constraint(diag_blocks, pltpu.HBM),
    )
    other = swap(own, 1)
    both = jnp.concatenate([own, other])
    first, fourth = across(both, 1), across(both, 4)
    halves = half_products(barrier((bases, other))[0], near_blocks)
    halves, first, fourth = barrier((halves, first, fourth))
    first_other, fourth_other = swap(first, 1), swap(fourth, 1)
    second = across(first_other, 1)
    third = around(ring_package(both, fourth))
    rows, exchange, part = inner(
        leaf_nbrs, shift, halves, skeleton, (own, other, first, first_other, fourth, fourth_other)
    )
    received = [swap(exchange[m - 1], m) for m in range(1, 4)]
    merged = outer(leaf_nbrs, parent_nbrs.T, part)
    merged, second, third, *received = barrier((merged, second, third, *received))
    merged, parent_block = last(
        leaf_nbrs, parent_nbrs.T, shift, halves, rows, received,
        (second, swap(second, 1), third, swap(third, 1)), merged,
    )
    return (leaf_factor, leaf_panel, merged, parent_block)


def solution(mesh):
    in_specs = (
        P("leaf", None, None, None),
        P("leaf", None, None),
        P("leaf", None, None),
        P("leaf", None),
        P(),
    )
    out_specs = (
        P("leaf", None, None),
        P("leaf", None, None),
        P("leaf", None, None, None),
        P("leaf", None),
    )
    return jax.shard_map(local, mesh=mesh, in_specs=in_specs, out_specs=out_specs, check_vma=False)
```

time: 97.6 us -> 59.4 us (0.61)
  the two profiles are of different devices: /device:TPU:1 before, /device:TPU:7 now
where the time goes in v2:
time: 59.4 us; the launch traced here: 59.3 us
  starting transfers between devices  22.4 us (38%)
  Pallas kernels  21.4 us (36%)
  waiting for transfers between devices  14.6 us (25%)
  between operations  0.91 us (2%)
    ppermute x8, starting transfers between devices, swap(): return lax.ppermute(value, 'leaf', pairs)  14.4 us
    ppermute x8, waiting for transfers between devices, swap(): return lax.ppermute(value, 'leaf', pairs)  9.66 us
    ppermute x3, starting transfers between devices, across(): return lax.ppermute(value, 'leaf', matched + [(b, a) for a, b in matched])  7.87 us
    pallas_call x1, Pallas kernels, k0(): pl.pallas_call(k0_body, in_specs=[pl.BlockSpec(memory_space=pltpu.HBM)] *...  7.56 us
    ppermute x3, waiting for transfers between devices, across(): return lax.ppermute(value, 'leaf', matched + [(b, a) for a, b in matched])  4.89 us
    pallas_call x1, Pallas kernels, last(): pl.pallas_call(last_body, in_specs=[pl.BlockSpec(memory_space=pltpu.SMEM)...  4.74 us
    pallas_call x1, Pallas kernels, outer(): pl.pallas_call(outer_body, in_specs=[pl.BlockSpec(memory_space=pltpu.SMEM...  3.86 us
    pallas_call x1, Pallas kernels, inner(): pl.pallas_call(inner_body, in_specs=[pl.BlockSpec(memory_space=pltpu.SMEM...  3.22 us
  transfers between devices with their start and end apart: 12, of which 7 were waited for; matrix products, arithmetic and copies ran while one was open for 0% of the time, Pallas kernels for 15%

profile of v2, /device:TPU:7, one launch (start us, length us, event | category | flops | bytes accessed | tf_op | source)
XLA Modules:
  0.0 59.3 jit_solution(2563241406815490022)
XLA Ops:
  0.7 7.6 %leaf_elimination.1 = (f32[2,128,128]{2,1,0:T(8,128)}, f32[2,128,128]{2,1,0:T(8,128)}, f32[2,128,128]{2,1,0:T(8,128)S(1)}, bf16[2,128,128]{2,1,0:T(8,128)(2,1)S(1)}, bf16[2,256,256]{2,1,0:T(8,128)(2,1)S(1)}) custom-call(bf16[2,256,256]{2,1,0:T(8,128)(2,1)} %u_ref, bf16[2,256,256]{2,1,0:T(8,128)(2,1)} %a_hbm.1), custom_call_target="tpu_custom_call" | custom-call | flops 7150000128 | tf_op jit(solution)/shard_map/leaf_elimination/pallas_call | solution.py:144
  8.2 0.8 %collective-permute-start = (bf16[2,256,256]{2,1,0:T(8,128)(2,1)S(1)}, bf16[2,256,256]{2,1,0:T(8,128)(2,1)S(1)}, u32[]{:S(2)}, u32[]{:S(2)}) collective-permute-start(bf16[2,256,256]{2,1,0:T(8,128)(2,1)S(1)} %get-tuple-element.27.refs_0_), channel_id=1, source_target_pairs={{0,1},{1,0},{2,3},{3,2},{4,5},{5,4},{6,7},{7,6},{8,9},{9,8},{10,11... | collective-permute-start | bytes 786440 | tf_op jit(solution)/shard_map/ppermute | solution.py:425
  9.0 1.1 %collective-permute-done.refs_1_ = bf16[2,256,256]{2,1,0:T(8,128)(2,1)S(1)} collective-permute-done((bf16[2,256,256]{2,1,0:T(8,128)(2,1)S(1)}, bf16[2,256,256]{2,1,0:T(8,128)(2,1)S(1)}, u32[]{:S(2)}, u32[]{:S(2)}) %collective-permute-start) | collective-permute-done | bytes 262176 | tf_op jit(solution)/shard_map/ppermute | solution.py:425
  10.2 0.0 copy-start.1
  10.2 2.0 %collective-permute-start.2 = (bf16[4,256,256]{2,1,0:T(8,128)(2,1)S(1)}, bf16[4,256,256]{2,1,0:T(8,128)(2,1)S(1)}, u32[]{:S(2)}, u32[]{:S(2)}) collective-permute-start(bf16[4,256,256]{2,1,0:T(8,128)(2,1)S(1)} %constant_dynamic-update-slice_fusion.own_ref), channel_id=1, source_target_pairs={{1,8},{3,10},{5,12},{7,14},{9,16},{11,18},{13,20},{15,22},{17,24},... | collective-permute-start | bytes 1572872 | tf_op jit(solution)/shard_map/ppermute | solution.py:438
  12.2 5.5 %collective-permute-start.1 = (bf16[4,256,256]{2,1,0:T(8,128)(2,1)S(1)}, bf16[4,256,256]{2,1,0:T(8,128)(2,1)S(1)}, u32[]{:S(2)}, u32[]{:S(2)}) collective-permute-start(bf16[4,256,256]{2,1,0:T(8,128)(2,1)S(1)} %constant_dynamic-update-slice_fusion.own_ref), channel_id=1, source_target_pairs={{1,2},{3,4},{5,6},{7,8},{9,10},{11,12},{13,14},{15,16},{17,18},{19... | collective-permute-start | bytes 1572872 | tf_op jit(solution)/shard_map/ppermute | solution.py:438
  17.7 2.0 %half_products.1.h_ref = bf16[2,26,256,256]{3,2,1,0:T(8,128)(2,1)S(1)} custom-call(bf16[2,256,256]{2,1,0:T(8,128)(2,1)S(1)} %copy-done.3, bf16[2,26,256,256]{3,2,1,0:T(8,128)(2,1)S(1)} %copy-done.2), custom_call_target="tpu_custom_call" | custom-call | flops 3849999872 | tf_op jit(solution)/shard_map/half_products/pallas_call | solution.py:231
  19.6 0.0 collective-permute-done.2.refs_4_.far_ref
  19.7 4.9 %collective-permute-done.1.refs_2_ = bf16[4,256,256]{2,1,0:T(8,128)(2,1)S(1)} collective-permute-done((bf16[4,256,256]{2,1,0:T(8,128)(2,1)S(1)}, bf16[4,256,256]{2,1,0:T(8,128)(2,1)S(1)}, u32[]{:S(2)}, u32[]{:S(2)}) %collective-permute-start.1) | collective-permute-done | bytes 524320 | tf_op jit(solution)/shard_map/ppermute | solution.py:438
  24.5 6.9 %collective-permute-start.3 = (bf16[4,256,256]{2,1,0:T(8,128)(2,1)S(1)}, bf16[4,256,256]{2,1,0:T(8,128)(2,1)S(1)}, u32[]{:S(2)}, u32[]{:S(2)}) collective-permute-start(bf16[4,256,256]{2,1,0:T(8,128)(2,1)S(1)} %collective-permute-done.1.refs_2_), channel_id=1, source_target_pairs={{0,1},{1,0},{2,3},{3,2},{4,5},{5,4},{6,7},{7,6},{8,9},{9,8},{10,11... | collective-permute-start | bytes 1572872 | tf_op jit(solution)/shard_map/ppermute | solution.py:425
  31.4 0.0 collective-permute-start.4
  31.5 0.0 copy-start
  31.5 0.1 collective-permute-start.6
  31.6 1.4 %collective-permute-done.3.refs_3_ = bf16[4,256,256]{2,1,0:T(8,128)(2,1)S(1)} collective-permute-done((bf16[4,256,256]{2,1,0:T(8,128)(2,1)S(1)}, bf16[4,256,256]{2,1,0:T(8,128)(2,1)S(1)}, u32[]{:S(2)}, u32[]{:S(2)}) %collective-permute-start.3) | collective-permute-done | bytes 524320 | tf_op jit(solution)/shard_map/ppermute | solution.py:425
  33.0 0.4 collective-permute-start.5
  33.3 0.4 collective-permute-done.4.refs_5_
  33.7 3.2 %inner_rows.1 = (f32[2,128,1152]{2,1,0:T(8,128)S(1)}, bf16[3,256,256]{2,1,0:T(8,128)(2,1)S(1)}, f32[2,20,128,128]{3,2,1,0:T(8,128)S(1)}) custom-call(s32[2,26]{1,0:T(2,128)S(1)} %copy-done.1, bf16[2,128,128]{2,1,0:T(8,128)(2,1)S(1)} %get-tuple-element.26.s_ref, bf16[2,26,256,256]{3,2,1,0:T(8,128)(2,1)S(1)} %half_products.1.h_ref, ...), custom_call_target="tpu_custom_call" | custom-call | flops 11000000 | tf_op jit(solution)/shard_map/inner_rows/pallas_call | solution.py:276
  37.0 1.1 %collective-permute-start.9 = (bf16[256,256]{1,0:T(8,128)(2,1)S(1)}, bf16[256,256]{1,0:T(8,128)(2,1)S(1)}, u32[]{:S(2)}, u32[]{:S(2)}) collective-permute-start(bf16[256,256]{1,0:T(8,128)(2,1)S(1)} %get-tuple-element.44), channel_id=1, source_target_pairs={{0,3},{1,2},{2,1},{3,0},{4,7},{5,6},{6,5},{7,4},{8,11},{9,10},{10,... | collective-permute-start | bytes 393224 | tf_op jit(solution)/shard_map/ppermute | solution.py:425
  38.1 3.5 %collective-permute-start.8 = (bf16[256,256]{1,0:T(8,128)(2,1)S(1)}, bf16[256,256]{1,0:T(8,128)(2,1)S(1)}, u32[]{:S(2)}, u32[]{:S(2)}) collective-permute-start(bf16[256,256]{1,0:T(8,128)(2,1)S(1)} %get-tuple-element.45), channel_id=1, source_target_pairs={{0,2},{1,3},{2,0},{3,1},{4,6},{5,7},{6,4},{7,5},{8,10},{9,11},{10,... | collective-permute-start | bytes 393224 | tf_op jit(solution)/shard_map/ppermute | solution.py:425
  41.6 0.0 collective-permute-start.7
  41.6 0.0 copy-done
  41.6 3.9 %outer_rows.1.refs_4_ = f32[2,5,128,1024]{3,2,1,0:T(8,128)} custom-call(s32[2,26]{1,0:T(2,128)S(1)} %copy-done.1, s32[5,64]{1,0:T(8,128)S(1)} %bitcast.7, f32[2,20,128,128]{3,2,1,0:T(8,128)S(1)} %get-tuple-element.34.part_ref), custom_call_target="tpu_custom_call" | custom-call | flops 11000000 | tf_op jit(solution)/shard_map/outer_rows/pallas_call | solution.py:317
  45.4 0.0 collective-permute-done.6.refs_2_
  45.4 4.6 %collective-permute-done.9.r3_ref = bf16[256,256]{1,0:T(8,128)(2,1)S(1)} collective-permute-done((bf16[256,256]{1,0:T(8,128)(2,1)S(1)}, bf16[256,256]{1,0:T(8,128)(2,1)S(1)}, u32[]{:S(2)}, u32[]{:S(2)}) %collective-permute-start.9) | collective-permute-done | bytes 131104 | tf_op jit(solution)/shard_map/ppermute | solution.py:425
  50.0 0.0 collective-permute-done.8.r2_ref
  50.0 0.0 collective-permute-done.7.r1_ref
  50.0 0.0 collective-permute-done.5.refs_0_
  50.0 2.1 %collective-permute-start.10 = (bf16[4,256,256]{2,1,0:T(8,128)(2,1)S(1)}, bf16[4,256,256]{2,1,0:T(8,128)(2,1)S(1)}, u32[]{:S(2)}, u32[]{:S(2)}) collective-permute-start(bf16[4,256,256]{2,1,0:T(8,128)(2,1)S(1)} %collective-permute-done.5.refs_0_), channel_id=1, source_target_pairs={{0,1},{1,0},{2,3},{3,2},{4,5},{5,4},{6,7},{7,6},{8,9},{9,8},{10,11... | collective-permute-start | bytes 1572872 | tf_op jit(solution)/shard_map/ppermute | solution.py:425
  52.1 0.1 collective-permute-start.11
  52.2 1.4 %collective-permute-done.10.refs_1_ = bf16[4,256,256]{2,1,0:T(8,128)(2,1)S(1)} collective-permute-done((bf16[4,256,256]{2,1,0:T(8,128)(2,1)S(1)}, bf16[4,256,256]{2,1,0:T(8,128)(2,1)S(1)}, u32[]{:S(2)}, u32[]{:S(2)}) %collective-permute-start.10) | collective-permute-done | bytes 524320 | tf_op jit(solution)/shard_map/ppermute | solution.py:425
  53.7 0.7 %collective-permute-done.11.refs_3_ = bf16[4,256,256]{2,1,0:T(8,128)(2,1)S(1)} collective-permute-done((bf16[4,256,256]{2,1,0:T(8,128)(2,1)S(1)}, bf16[4,256,256]{2,1,0:T(8,128)(2,1)S(1)}, u32[]{:S(2)}, u32[]{:S(2)}) %collective-permute-start.11) | collective-permute-done | bytes 524320 | tf_op jit(solution)/shard_map/ppermute | solution.py:425
  54.4 4.7 %last_rows.1 = (f32[2,5,128,1024]{3,2,1,0:T(8,128)}, f32[256,1024]{1,0:T(8,128)}) custom-call(s32[2,26]{1,0:T(2,128)S(1)} %copy-done.1, s32[5,64]{1,0:T(8,128)S(1)} %bitcast.8, bf16[2,128,128]{2,1,0:T(8,128)(2,1)S(1)} %get-tuple-element.26.s_ref, bf16[2,26,256,256]{3,2,1,0:T(8,128)(2,1)S(1)} %half_products.1.h_ref, ...), custom_call_target="tpu_custom_call", output_to_operand_aliasing={{0}: (12, {})} | custom-call | flops 11000000 | tf_op jit(solution)/shard_map/last_rows/pallas_call | solution.py:375
  (9 shorter events, 0.1 us)
Async XLA Ops:
  0.6 17.0 %copy-start.3 = (bf16[2,256,256]{2,1,0:T(8,128)(2,1)S(1)}, bf16[2,256,256]{2,1,0:T(8,128)(2,1)}, u32[]{:S(2)}) copy-start(bf16[2,256,256]{2,1,0:T(8,128)(2,1)} %u_ref) | copy-start | bytes 786436
  0.6 17.0 %copy-start.2 = (bf16[2,26,256,256]{3,2,1,0:T(8,128)(2,1)S(1)}, bf16[2,26,256,256]{3,2,1,0:T(8,128)(2,1)}, u32[]{:S(2)}) copy-start(bf16[2,26,256,256]{3,2,1,0:T(8,128)(2,1)} %a_ref.1) | copy-start | bytes 20447236
  8.2 1.9 %collective-permute-start = (bf16[2,256,256]{2,1,0:T(8,128)(2,1)S(1)}, bf16[2,256,256]{2,1,0:T(8,128)(2,1)S(1)}, u32[]{:S(2)}, u32[]{:S(2)}) collective-permute-start(bf16[2,256,256]{2,1,0:T(8,128)(2,1)S(1)} %get-tuple-element.27.refs_0_), channel_id=1, source_target_pairs={{0,1},{1,0},{2,3},{3,2},{4,5},{5,4},{6,7},{7,6},{8,9},{9,8},{10,11... | collective-permute-start | bytes 786440 | tf_op jit(solution)/shard_map/ppermute | solution.py:425
  10.2 23.6 %copy-start.1 = (s32[2,26]{1,0:T(2,128)S(1)}, s32[2,26]{1,0:T(2,128)}, u32[]{:S(2)}) copy-start(s32[2,26]{1,0:T(2,128)} %nbrs.5) | copy-start | bytes 628
  10.2 9.5 %collective-permute-start.2 = (bf16[4,256,256]{2,1,0:T(8,128)(2,1)S(1)}, bf16[4,256,256]{2,1,0:T(8,128)(2,1)S(1)}, u32[]{:S(2)}, u32[]{:S(2)}) collective-permute-start(bf16[4,256,256]{2,1,0:T(8,128)(2,1)S(1)} %constant_dynamic-update-slice_fusion.own_ref), channel_id=1, source_target_pairs={{1,8},{3,10},{5,12},{7,14},{9,16},{11,18},{13,20},{15,22},{17,24},... | collective-permute-start | bytes 1572872 | tf_op jit(solution)/shard_map/ppermute | solution.py:438
  12.2 12.4 %collective-permute-start.1 = (bf16[4,256,256]{2,1,0:T(8,128)(2,1)S(1)}, bf16[4,256,256]{2,1,0:T(8,128)(2,1)S(1)}, u32[]{:S(2)}, u32[]{:S(2)}) collective-permute-start(bf16[4,256,256]{2,1,0:T(8,128)(2,1)S(1)} %constant_dynamic-update-slice_fusion.own_ref), channel_id=1, source_target_pairs={{1,2},{3,4},{5,6},{7,8},{9,10},{11,12},{13,14},{15,16},{17,18},{19... | collective-permute-start | bytes 1572872 | tf_op jit(solution)/shard_map/ppermute | solution.py:438
  24.5 8.4 %collective-permute-start.3 = (bf16[4,256,256]{2,1,0:T(8,128)(2,1)S(1)}, bf16[4,256,256]{2,1,0:T(8,128)(2,1)S(1)}, u32[]{:S(2)}, u32[]{:S(2)}) collective-permute-start(bf16[4,256,256]{2,1,0:T(8,128)(2,1)S(1)} %collective-permute-done.1.refs_2_), channel_id=1, source_target_pairs={{0,1},{1,0},{2,3},{3,2},{4,5},{5,4},{6,7},{7,6},{8,9},{9,8},{10,11... | collective-permute-start | bytes 1572872 | tf_op jit(solution)/shard_map/ppermute | solution.py:425
  31.4 2.3 %collective-permute-start.4 = (bf16[4,256,256]{2,1,0:T(8,128)(2,1)S(1)}, bf16[4,256,256]{2,1,0:T(8,128)(2,1)S(1)}, u32[]{:S(2)}, u32[]{:S(2)}) collective-permute-start(bf16[4,256,256]{2,1,0:T(8,128)(2,1)S(1)} %collective-permute-done.2.refs_4_.far_ref), channel_id=1, source_target_pairs={{0,1},{1,0},{2,3},{3,2},{4,5},{5,4},{6,7},{7,6},{8,9},{9,8},{10,11... | collective-permute-start | bytes 1572872 | tf_op jit(solution)/shard_map/ppermute | solution.py:425
  31.5 10.1 %copy-start = (s32[64,5]{0,1:T(8,128)S(1)}, s32[64,5]{0,1:T(8,128)}, u32[]{:S(2)}) copy-start(s32[64,5]{0,1:T(8,128)} %param.9) | copy-start | bytes 3844
  31.5 13.9 %collective-permute-start.6 = (bf16[4,256,256]{2,1,0:T(8,128)(2,1)S(1)}, bf16[4,256,256]{2,1,0:T(8,128)(2,1)S(1)}, u32[]{:S(2)}, u32[]{:S(2)}) collective-permute-start(bf16[4,256,256]{2,1,0:T(8,128)(2,1)S(1)} %ring_package.1), channel_id=1, source_target_pairs={{1,2},{3,4},{5,6},{7,0},{9,10},{11,12},{13,14},{15,8},{17,18},{19,... | collective-permute-start | bytes 1572872 | tf_op jit(solution)/shard_map/ppermute | solution.py:446
  33.0 17.1 %collective-permute-start.5 = (bf16[4,256,256]{2,1,0:T(8,128)(2,1)S(1)}, bf16[4,256,256]{2,1,0:T(8,128)(2,1)S(1)}, u32[]{:S(2)}, u32[]{:S(2)}) collective-permute-start(bf16[4,256,256]{2,1,0:T(8,128)(2,1)S(1)} %collective-permute-done.3.refs_3_), channel_id=1, source_target_pairs={{1,2},{3,4},{5,6},{7,8},{9,10},{11,12},{13,14},{15,16},{17,18},{19... | collective-permute-start | bytes 1572872 | tf_op jit(solution)/shard_map/ppermute | solution.py:438
  37.0 13.0 %collective-permute-start.9 = (bf16[256,256]{1,0:T(8,128)(2,1)S(1)}, bf16[256,256]{1,0:T(8,128)(2,1)S(1)}, u32[]{:S(2)}, u32[]{:S(2)}) collective-permute-start(bf16[256,256]{1,0:T(8,128)(2,1)S(1)} %get-tuple-element.44), channel_id=1, source_target_pairs={{0,3},{1,2},{2,1},{3,0},{4,7},{5,6},{6,5},{7,4},{8,11},{9,10},{10,... | collective-permute-start | bytes 393224 | tf_op jit(solution)/shard_map/ppermute | solution.py:425
  38.1 12.0 %collective-permute-start.8 = (bf16[256,256]{1,0:T(8,128)(2,1)S(1)}, bf16[256,256]{1,0:T(8,128)(2,1)S(1)}, u32[]{:S(2)}, u32[]{:S(2)}) collective-permute-start(bf16[256,256]{1,0:T(8,128)(2,1)S(1)} %get-tuple-element.45), channel_id=1, source_target_pairs={{0,2},{1,3},{2,0},{3,1},{4,6},{5,7},{6,4},{7,5},{8,10},{9,11},{10,... | collective-permute-start | bytes 393224 | tf_op jit(solution)/shard_map/ppermute | solution.py:425
  41.6 8.5 %collective-permute-start.7 = (bf16[256,256]{1,0:T(8,128)(2,1)S(1)}, bf16[256,256]{1,0:T(8,128)(2,1)S(1)}, u32[]{:S(2)}, u32[]{:S(2)}) collective-permute-start(bf16[256,256]{1,0:T(8,128)(2,1)S(1)} %get-tuple-element.46), channel_id=1, source_target_pairs={{0,1},{1,0},{2,3},{3,2},{4,5},{5,4},{6,7},{7,6},{8,9},{9,8},{10,11... | collective-permute-start | bytes 393224 | tf_op jit(solution)/shard_map/ppermute | solution.py:425
  50.0 3.6 %collective-permute-start.10 = (bf16[4,256,256]{2,1,0:T(8,128)(2,1)S(1)}, bf16[4,256,256]{2,1,0:T(8,128)(2,1)S(1)}, u32[]{:S(2)}, u32[]{:S(2)}) collective-permute-start(bf16[4,256,256]{2,1,0:T(8,128)(2,1)S(1)} %collective-permute-done.5.refs_0_), channel_id=1, source_target_pairs={{0,1},{1,0},{2,3},{3,2},{4,5},{5,4},{6,7},{7,6},{8,9},{9,8},{10,11... | collective-permute-start | bytes 1572872 | tf_op jit(solution)/shard_map/ppermute | solution.py:425
  52.1 2.3 %collective-permute-start.11 = (bf16[4,256,256]{2,1,0:T(8,128)(2,1)S(1)}, bf16[4,256,256]{2,1,0:T(8,128)(2,1)S(1)}, u32[]{:S(2)}, u32[]{:S(2)}) collective-permute-start(bf16[4,256,256]{2,1,0:T(8,128)(2,1)S(1)} %collective-permute-done.6.refs_2_), channel_id=1, source_target_pairs={{0,1},{1,0},{2,3},{3,2},{4,5},{5,4},{6,7},{7,6},{8,9},{9,8},{10,11... | collective-permute-start | bytes 1572872 | tf_op jit(solution)/shard_map/ppermute | solution.py:425

commit v3 on v2

--- a/solution.py
+++ b/solution.py
@@ -465,10 +465,12 @@
     )
     received = [swap(exchange[m - 1], m) for m in range(1, 4)]
     merged = outer(leaf_nbrs, parent_nbrs.T, part)
-    merged, second, third, *received = barrier((merged, second, third, *received))
+    merged, third = barrier((merged, third))
+    third_other = swap(third, 1)
+    merged, second, *received = barrier((merged, second, *received))
     merged, parent_block = last(
         leaf_nbrs, parent_nbrs.T, shift, halves, rows, received,
-        (second, swap(second, 1), third, swap(third, 1)), merged,
+        (second, swap(second, 1), third, third_other), merged,
     )
     return (leaf_factor, leaf_panel, merged, parent_block)
 

time: 59.4 us -> 58.6 us (0.987)
  waiting for transfers between devices: 14.6 us -> 11.8 us
  starting transfers between devices: 22.4 us -> 24.4 us
    ppermute x8, waiting for transfers between devices: 9.66 us -> 6.92 us  [swap(): return lax.ppermute(value, 'leaf', pairs)]
    ppermute x8, starting transfers between devices: 14.4 us -> 16.4 us  [swap(): return lax.ppermute(value, 'leaf', pairs)]
  transfers between devices with their start and end apart: 12 -> 12, of which waited for: 7 -> 6; matrix products, arithmetic and copies ran while one was open for 0% -> 0% of each run, Pallas kernels for 15% -> 16%
where the time goes in v3:
time: 58.6 us
  starting transfers between devices  24.4 us (42%)
  Pallas kernels  21.4 us (37%)
  waiting for transfers between devices  11.8 us (20%)
  between operations  0.91 us (2%)
    ppermute x8, starting transfers between devices, swap(): return lax.ppermute(value, 'leaf', pairs)  16.4 us
    ppermute x3, starting transfers between devices, across(): return lax.ppermute(value, 'leaf', matched + [(b, a) for a, b in matched])  7.87 us
    pallas_call x1, Pallas kernels, k0(): pl.pallas_call(k0_body, in_specs=[pl.BlockSpec(memory_space=pltpu.HBM)] *...  7.56 us
    ppermute x8, waiting for transfers between devices, swap(): return lax.ppermute(value, 'leaf', pairs)  6.92 us
    ppermute x3, waiting for transfers between devices, across(): return lax.ppermute(value, 'leaf', matched + [(b, a) for a, b in matched])  4.89 us
    pallas_call x1, Pallas kernels, last(): pl.pallas_call(last_body, in_specs=[pl.BlockSpec(memory_space=pltpu.SMEM)...  4.77 us
    pallas_call x1, Pallas kernels, outer(): pl.pallas_call(outer_body, in_specs=[pl.BlockSpec(memory_space=pltpu.SMEM...  3.86 us
    pallas_call x1, Pallas kernels, inner(): pl.pallas_call(inner_body, in_specs=[pl.BlockSpec(memory_space=pltpu.SMEM...  3.22 us
  transfers between devices with their start and end apart: 12, of which 6 were waited for; matrix products, arithmetic and copies ran while one was open for 0% of the time, Pallas kernels for 16%

profile of v3, /device:TPU:7, one launch (start us, length us, event | category | flops | bytes accessed | tf_op | source)
XLA Modules:
  0.0 58.6 jit_solution(16057281258330016333)
XLA Ops:
  0.6 0.0 copy-start.3
  0.7 7.6 %leaf_elimination.1 = (f32[2,128,128]{2,1,0:T(8,128)}, f32[2,128,128]{2,1,0:T(8,128)}, f32[2,128,128]{2,1,0:T(8,128)S(1)}, bf16[2,128,128]{2,1,0:T(8,128)(2,1)S(1)}, bf16[2,256,256]{2,1,0:T(8,128)(2,1)S(1)}) custom-call(bf16[2,256,256]{2,1,0:T(8,128)(2,1)} %u_ref, bf16[2,256,256]{2,1,0:T(8,128)(2,1)} %a_hbm.1), custom_call_target="tpu_custom_call" | custom-call | flops 7150000128 | tf_op jit(solution)/shard_map/leaf_elimination/pallas_call | solution.py:144
  8.2 0.8 %collective-permute-start = (bf16[2,256,256]{2,1,0:T(8,128)(2,1)S(1)}, bf16[2,256,256]{2,1,0:T(8,128)(2,1)S(1)}, u32[]{:S(2)}, u32[]{:S(2)}) collective-permute-start(bf16[2,256,256]{2,1,0:T(8,128)(2,1)S(1)} %get-tuple-element.28.refs_0_), channel_id=1, source_target_pairs={{0,1},{1,0},{2,3},{3,2},{4,5},{5,4},{6,7},{7,6},{8,9},{9,8},{10,11... | collective-permute-start | bytes 786440 | tf_op jit(solution)/shard_map/ppermute | solution.py:425
  9.0 1.1 %collective-permute-done.refs_1_ = bf16[2,256,256]{2,1,0:T(8,128)(2,1)S(1)} collective-permute-done((bf16[2,256,256]{2,1,0:T(8,128)(2,1)S(1)}, bf16[2,256,256]{2,1,0:T(8,128)(2,1)S(1)}, u32[]{:S(2)}, u32[]{:S(2)}) %collective-permute-start) | collective-permute-done | bytes 262176 | tf_op jit(solution)/shard_map/ppermute | solution.py:425
  10.2 0.0 copy-start.1
  10.2 2.0 %collective-permute-start.2 = (bf16[4,256,256]{2,1,0:T(8,128)(2,1)S(1)}, bf16[4,256,256]{2,1,0:T(8,128)(2,1)S(1)}, u32[]{:S(2)}, u32[]{:S(2)}) collective-permute-start(bf16[4,256,256]{2,1,0:T(8,128)(2,1)S(1)} %constant_dynamic-update-slice_fusion.own_ref), channel_id=1, source_target_pairs={{1,8},{3,10},{5,12},{7,14},{9,16},{11,18},{13,20},{15,22},{17,24},... | collective-permute-start | bytes 1572872 | tf_op jit(solution)/shard_map/ppermute | solution.py:438
  12.2 5.5 %collective-permute-start.1 = (bf16[4,256,256]{2,1,0:T(8,128)(2,1)S(1)}, bf16[4,256,256]{2,1,0:T(8,128)(2,1)S(1)}, u32[]{:S(2)}, u32[]{:S(2)}) collective-permute-start(bf16[4,256,256]{2,1,0:T(8,128)(2,1)S(1)} %constant_dynamic-update-slice_fusion.own_ref), channel_id=1, source_target_pairs={{1,2},{3,4},{5,6},{7,8},{9,10},{11,12},{13,14},{15,16},{17,18},{19... | collective-permute-start | bytes 1572872 | tf_op jit(solution)/shard_map/ppermute | solution.py:438
  17.7 2.0 %half_products.1.h_ref = bf16[2,26,256,256]{3,2,1,0:T(8,128)(2,1)S(1)} custom-call(bf16[2,256,256]{2,1,0:T(8,128)(2,1)S(1)} %copy-done.3, bf16[2,26,256,256]{3,2,1,0:T(8,128)(2,1)S(1)} %copy-done.2), custom_call_target="tpu_custom_call" | custom-call | flops 3849999872 | tf_op jit(solution)/shard_map/half_products/pallas_call | solution.py:231
  19.6 0.0 collective-permute-done.2.refs_4_.far_ref
  19.7 4.9 %collective-permute-done.1.refs_2_ = bf16[4,256,256]{2,1,0:T(8,128)(2,1)S(1)} collective-permute-done((bf16[4,256,256]{2,1,0:T(8,128)(2,1)S(1)}, bf16[4,256,256]{2,1,0:T(8,128)(2,1)S(1)}, u32[]{:S(2)}, u32[]{:S(2)}) %collective-permute-start.1) | collective-permute-done | bytes 524320 | tf_op jit(solution)/shard_map/ppermute | solution.py:438
  24.5 6.9 %collective-permute-start.3 = (bf16[4,256,256]{2,1,0:T(8,128)(2,1)S(1)}, bf16[4,256,256]{2,1,0:T(8,128)(2,1)S(1)}, u32[]{:S(2)}, u32[]{:S(2)}) collective-permute-start(bf16[4,256,256]{2,1,0:T(8,128)(2,1)S(1)} %collective-permute-done.1.refs_2_), channel_id=1, source_target_pairs={{0,1},{1,0},{2,3},{3,2},{4,5},{5,4},{6,7},{7,6},{8,9},{9,8},{10,11... | collective-permute-start | bytes 1572872 | tf_op jit(solution)/shard_map/ppermute | solution.py:425
  31.4 0.0 collective-permute-start.4
  31.5 0.0 copy-start
  31.5 0.1 collective-permute-start.5
  31.6 1.4 %collective-permute-done.3.refs_3_ = bf16[4,256,256]{2,1,0:T(8,128)(2,1)S(1)} collective-permute-done((bf16[4,256,256]{2,1,0:T(8,128)(2,1)S(1)}, bf16[4,256,256]{2,1,0:T(8,128)(2,1)S(1)}, u32[]{:S(2)}, u32[]{:S(2)}) %collective-permute-start.3) | collective-permute-done | bytes 524320 | tf_op jit(solution)/shard_map/ppermute | solution.py:425
  33.0 0.4 collective-permute-start.6
  33.3 0.4 collective-permute-done.4.refs_5_
  33.7 3.2 %inner_rows.1 = (f32[2,128,1152]{2,1,0:T(8,128)S(1)}, bf16[3,256,256]{2,1,0:T(8,128)(2,1)S(1)}, f32[2,20,128,128]{3,2,1,0:T(8,128)S(1)}) custom-call(s32[2,26]{1,0:T(2,128)S(1)} %copy-done.1, bf16[2,128,128]{2,1,0:T(8,128)(2,1)S(1)} %get-tuple-element.27.s_ref, bf16[2,26,256,256]{3,2,1,0:T(8,128)(2,1)S(1)} %half_products.1.h_ref, ...), custom_call_target="tpu_custom_call" | custom-call | flops 11000000 | tf_op jit(solution)/shard_map/inner_rows/pallas_call | solution.py:276
  37.0 1.1 %collective-permute-start.9 = (bf16[256,256]{1,0:T(8,128)(2,1)S(1)}, bf16[256,256]{1,0:T(8,128)(2,1)S(1)}, u32[]{:S(2)}, u32[]{:S(2)}) collective-permute-start(bf16[256,256]{1,0:T(8,128)(2,1)S(1)} %get-tuple-element.46), channel_id=1, source_target_pairs={{0,3},{1,2},{2,1},{3,0},{4,7},{5,6},{6,5},{7,4},{8,11},{9,10},{10,... | collective-permute-start | bytes 393224 | tf_op jit(solution)/shard_map/ppermute | solution.py:425
  38.1 3.5 %collective-permute-start.8 = (bf16[256,256]{1,0:T(8,128)(2,1)S(1)}, bf16[256,256]{1,0:T(8,128)(2,1)S(1)}, u32[]{:S(2)}, u32[]{:S(2)}) collective-permute-start(bf16[256,256]{1,0:T(8,128)(2,1)S(1)} %get-tuple-element.47), channel_id=1, source_target_pairs={{0,2},{1,3},{2,0},{3,1},{4,6},{5,7},{6,4},{7,5},{8,10},{9,11},{10,... | collective-permute-start | bytes 393224 | tf_op jit(solution)/shard_map/ppermute | solution.py:425
  41.6 0.0 collective-permute-start.7
  41.6 3.9 %outer_rows.1.refs_4_ = f32[2,5,128,1024]{3,2,1,0:T(8,128)} custom-call(s32[2,26]{1,0:T(2,128)S(1)} %copy-done.1, s32[5,64]{1,0:T(8,128)S(1)} %bitcast.7, f32[2,20,128,128]{3,2,1,0:T(8,128)S(1)} %get-tuple-element.35.part_ref), custom_call_target="tpu_custom_call" | custom-call | flops 11000000 | tf_op jit(solution)/shard_map/outer_rows/pallas_call | solution.py:317
  45.4 0.0 collective-permute-done.5.refs_2_
  45.4 2.1 %collective-permute-start.11 = (bf16[4,256,256]{2,1,0:T(8,128)(2,1)S(1)}, bf16[4,256,256]{2,1,0:T(8,128)(2,1)S(1)}, u32[]{:S(2)}, u32[]{:S(2)}) collective-permute-start(bf16[4,256,256]{2,1,0:T(8,128)(2,1)S(1)} %collective-permute-done.5.refs_2_), channel_id=1, source_target_pairs={{0,1},{1,0},{2,3},{3,2},{4,5},{5,4},{6,7},{7,6},{8,9},{9,8},{10,11... | collective-permute-start | bytes 1572872 | tf_op jit(solution)/shard_map/ppermute | solution.py:425
  47.5 2.5 %collective-permute-done.9.r3_ref = bf16[256,256]{1,0:T(8,128)(2,1)S(1)} collective-permute-done((bf16[256,256]{1,0:T(8,128)(2,1)S(1)}, bf16[256,256]{1,0:T(8,128)(2,1)S(1)}, u32[]{:S(2)}, u32[]{:S(2)}) %collective-permute-start.9) | collective-permute-done | bytes 131104 | tf_op jit(solution)/shard_map/ppermute | solution.py:425
  50.0 0.0 collective-permute-done.8.r2_ref
  50.0 0.0 collective-permute-done.7.r1_ref
  50.0 0.0 collective-permute-done.6.refs_0_
  50.0 2.1 %collective-permute-start.10 = (bf16[4,256,256]{2,1,0:T(8,128)(2,1)S(1)}, bf16[4,256,256]{2,1,0:T(8,128)(2,1)S(1)}, u32[]{:S(2)}, u32[]{:S(2)}) collective-permute-start(bf16[4,256,256]{2,1,0:T(8,128)(2,1)S(1)} %collective-permute-done.6.refs_0_), channel_id=1, source_target_pairs={{0,1},{1,0},{2,3},{3,2},{4,5},{5,4},{6,7},{7,6},{8,9},{9,8},{10,11... | collective-permute-start | bytes 1572872 | tf_op jit(solution)/shard_map/ppermute | solution.py:425
  52.1 0.0 collective-permute-done.11.refs_3_
  52.1 1.5 %collective-permute-done.10.refs_1_ = bf16[4,256,256]{2,1,0:T(8,128)(2,1)S(1)} collective-permute-done((bf16[4,256,256]{2,1,0:T(8,128)(2,1)S(1)}, bf16[4,256,256]{2,1,0:T(8,128)(2,1)S(1)}, u32[]{:S(2)}, u32[]{:S(2)}) %collective-permute-start.10) | collective-permute-done | bytes 524320 | tf_op jit(solution)/shard_map/ppermute | solution.py:425
  53.7 4.8 %last_rows.1 = (f32[2,5,128,1024]{3,2,1,0:T(8,128)}, f32[256,1024]{1,0:T(8,128)}) custom-call(s32[2,26]{1,0:T(2,128)S(1)} %copy-done.1, s32[5,64]{1,0:T(8,128)S(1)} %bitcast.8, bf16[2,128,128]{2,1,0:T(8,128)(2,1)S(1)} %get-tuple-element.27.s_ref, bf16[2,26,256,256]{3,2,1,0:T(8,128)(2,1)S(1)} %half_products.1.h_ref, ...), custom_call_target="tpu_custom_call", output_to_operand_aliasing={{0}: (12, {})} | custom-call | flops 11000000 | tf_op jit(solution)/shard_map/last_rows/pallas_call | solution.py:375
  (9 shorter events, 0.1 us)
Async XLA Ops:
  0.6 17.0 %copy-start.3 = (bf16[2,256,256]{2,1,0:T(8,128)(2,1)S(1)}, bf16[2,256,256]{2,1,0:T(8,128)(2,1)}, u32[]{:S(2)}) copy-start(bf16[2,256,256]{2,1,0:T(8,128)(2,1)} %u_ref) | copy-start | bytes 786436
  0.6 17.0 %copy-start.2 = (bf16[2,26,256,256]{3,2,1,0:T(8,128)(2,1)S(1)}, bf16[2,26,256,256]{3,2,1,0:T(8,128)(2,1)}, u32[]{:S(2)}) copy-start(bf16[2,26,256,256]{3,2,1,0:T(8,128)(2,1)} %a_ref.1) | copy-start | bytes 20447236
  8.2 1.9 %collective-permute-start = (bf16[2,256,256]{2,1,0:T(8,128)(2,1)S(1)}, bf16[2,256,256]{2,1,0:T(8,128)(2,1)S(1)}, u32[]{:S(2)}, u32[]{:S(2)}) collective-permute-start(bf16[2,256,256]{2,1,0:T(8,128)(2,1)S(1)} %get-tuple-element.28.refs_0_), channel_id=1, source_target_pairs={{0,1},{1,0},{2,3},{3,2},{4,5},{5,4},{6,7},{7,6},{8,9},{9,8},{10,11... | collective-permute-start | bytes 786440 | tf_op jit(solution)/shard_map/ppermute | solution.py:425
  10.2 23.6 %copy-start.1 = (s32[2,26]{1,0:T(2,128)S(1)}, s32[2,26]{1,0:T(2,128)}, u32[]{:S(2)}) copy-start(s32[2,26]{1,0:T(2,128)} %nbrs.5) | copy-start | bytes 628
  10.2 9.5 %collective-permute-start.2 = (bf16[4,256,256]{2,1,0:T(8,128)(2,1)S(1)}, bf16[4,256,256]{2,1,0:T(8,128)(2,1)S(1)}, u32[]{:S(2)}, u32[]{:S(2)}) collective-permute-start(bf16[4,256,256]{2,1,0:T(8,128)(2,1)S(1)} %constant_dynamic-update-slice_fusion.own_ref), channel_id=1, source_target_pairs={{1,8},{3,10},{5,12},{7,14},{9,16},{11,18},{13,20},{15,22},{17,24},... | collective-permute-start | bytes 1572872 | tf_op jit(solution)/shard_map/ppermute | solution.py:438
  12.2 12.4 %collective-permute-start.1 = (bf16[4,256,256]{2,1,0:T(8,128)(2,1)S(1)}, bf16[4,256,256]{2,1,0:T(8,128)(2,1)S(1)}, u32[]{:S(2)}, u32[]{:S(2)}) collective-permute-start(bf16[4,256,256]{2,1,0:T(8,128)(2,1)S(1)} %constant_dynamic-update-slice_fusion.own_ref), channel_id=1, source_target_pairs={{1,2},{3,4},{5,6},{7,8},{9,10},{11,12},{13,14},{15,16},{17,18},{19... | collective-permute-start | bytes 1572872 | tf_op jit(solution)/shard_map/ppermute | solution.py:438
  24.5 8.4 %collective-permute-start.3 = (bf16[4,256,256]{2,1,0:T(8,128)(2,1)S(1)}, bf16[4,256,256]{2,1,0:T(8,128)(2,1)S(1)}, u32[]{:S(2)}, u32[]{:S(2)}) collective-permute-start(bf16[4,256,256]{2,1,0:T(8,128)(2,1)S(1)} %collective-permute-done.1.refs_2_), channel_id=1, source_target_pairs={{0,1},{1,0},{2,3},{3,2},{4,5},{5,4},{6,7},{7,6},{8,9},{9,8},{10,11... | collective-permute-start | bytes 1572872 | tf_op jit(solution)/shard_map/ppermute | solution.py:425
  31.4 2.3 %collective-permute-start.4 = (bf16[4,256,256]{2,1,0:T(8,128)(2,1)S(1)}, bf16[4,256,256]{2,1,0:T(8,128)(2,1)S(1)}, u32[]{:S(2)}, u32[]{:S(2)}) collective-permute-start(bf16[4,256,256]{2,1,0:T(8,128)(2,1)S(1)} %collective-permute-done.2.refs_4_.far_ref), channel_id=1, source_target_pairs={{0,1},{1,0},{2,3},{3,2},{4,5},{5,4},{6,7},{7,6},{8,9},{9,8},{10,11... | collective-permute-start | bytes 1572872 | tf_op jit(solution)/shard_map/ppermute | solution.py:425
  31.5 10.1 %copy-start = (s32[64,5]{0,1:T(8,128)S(1)}, s32[64,5]{0,1:T(8,128)}, u32[]{:S(2)}) copy-start(s32[64,5]{0,1:T(8,128)} %param.9) | copy-start | bytes 3844
  31.5 13.9 %collective-permute-start.5 = (bf16[4,256,256]{2,1,0:T(8,128)(2,1)S(1)}, bf16[4,256,256]{2,1,0:T(8,128)(2,1)S(1)}, u32[]{:S(2)}, u32[]{:S(2)}) collective-permute-start(bf16[4,256,256]{2,1,0:T(8,128)(2,1)S(1)} %ring_package.1), channel_id=1, source_target_pairs={{1,2},{3,4},{5,6},{7,0},{9,10},{11,12},{13,14},{15,8},{17,18},{19,... | collective-permute-start | bytes 1572872 | tf_op jit(solution)/shard_map/ppermute | solution.py:446
  33.0 17.1 %collective-permute-start.6 = (bf16[4,256,256]{2,1,0:T(8,128)(2,1)S(1)}, bf16[4,256,256]{2,1,0:T(8,128)(2,1)S(1)}, u32[]{:S(2)}, u32[]{:S(2)}) collective-permute-start(bf16[4,256,256]{2,1,0:T(8,128)(2,1)S(1)} %collective-permute-done.3.refs_3_), channel_id=1, source_target_pairs={{1,2},{3,4},{5,6},{7,8},{9,10},{11,12},{13,14},{15,16},{17,18},{19... | collective-permute-start | bytes 1572872 | tf_op jit(solution)/shard_map/ppermute | solution.py:438
  37.0 13.0 %collective-permute-start.9 = (bf16[256,256]{1,0:T(8,128)(2,1)S(1)}, bf16[256,256]{1,0:T(8,128)(2,1)S(1)}, u32[]{:S(2)}, u32[]{:S(2)}) collective-permute-start(bf16[256,256]{1,0:T(8,128)(2,1)S(1)} %get-tuple-element.46), channel_id=1, source_target_pairs={{0,3},{1,2},{2,1},{3,0},{4,7},{5,6},{6,5},{7,4},{8,11},{9,10},{10,... | collective-permute-start | bytes 393224 | tf_op jit(solution)/shard_map/ppermute | solution.py:425
  38.1 12.0 %collective-permute-start.8 = (bf16[256,256]{1,0:T(8,128)(2,1)S(1)}, bf16[256,256]{1,0:T(8,128)(2,1)S(1)}, u32[]{:S(2)}, u32[]{:S(2)}) collective-permute-start(bf16[256,256]{1,0:T(8,128)(2,1)S(1)} %get-tuple-element.47), channel_id=1, source_target_pairs={{0,2},{1,3},{2,0},{3,1},{4,6},{5,7},{6,4},{7,5},{8,10},{9,11},{10,... | collective-permute-start | bytes 393224 | tf_op jit(solution)/shard_map/ppermute | solution.py:425
  41.6 8.5 %collective-permute-start.7 = (bf16[256,256]{1,0:T(8,128)(2,1)S(1)}, bf16[256,256]{1,0:T(8,128)(2,1)S(1)}, u32[]{:S(2)}, u32[]{:S(2)}) collective-permute-start(bf16[256,256]{1,0:T(8,128)(2,1)S(1)} %get-tuple-element.48), channel_id=1, source_target_pairs={{0,1},{1,0},{2,3},{3,2},{4,5},{5,4},{6,7},{7,6},{8,9},{9,8},{10,11... | collective-permute-start | bytes 393224 | tf_op jit(solution)/shard_map/ppermute | solution.py:425
  45.4 6.7 %collective-permute-start.11 = (bf16[4,256,256]{2,1,0:T(8,128)(2,1)S(1)}, bf16[4,256,256]{2,1,0:T(8,128)(2,1)S(1)}, u32[]{:S(2)}, u32[]{:S(2)}) collective-permute-start(bf16[4,256,256]{2,1,0:T(8,128)(2,1)S(1)} %collective-permute-done.5.refs_2_), channel_id=1, source_target_pairs={{0,1},{1,0},{2,3},{3,2},{4,5},{5,4},{6,7},{7,6},{8,9},{9,8},{10,11... | collective-permute-start | bytes 1572872 | tf_op jit(solution)/shard_map/ppermute | solution.py:425
  50.0 3.6 %collective-permute-start.10 = (bf16[4,256,256]{2,1,0:T(8,128)(2,1)S(1)}, bf16[4,256,256]{2,1,0:T(8,128)(2,1)S(1)}, u32[]{:S(2)}, u32[]{:S(2)}) collective-permute-start(bf16[4,256,256]{2,1,0:T(8,128)(2,1)S(1)} %collective-permute-done.6.refs_0_), channel_id=1, source_target_pairs={{0,1},{1,0},{2,3},{3,2},{4,5},{5,4},{6,7},{7,6},{8,9},{9,8},{10,11... | collective-permute-start | bytes 1572872 | tf_op jit(solution)/shard_map/ppermute | solution.py:425
